TPU v7x, 32 devices: a whole 2x2x4 slice. The times are simulated.
32 devices in a mesh: hop: 4 (over z), node: 8 (over y, x, core).
Axes of the slice: x: 2, y: 2, z: 4, core: 2. Of those that a mesh axis runs over, the one named last changes fastest.
Arguments:
- child_features: bfloat16 [16384, 1024], P(('hop', 'node')), may hold values from -6 to 6
- child_type: int32 [16384], P(('hop', 'node')), may hold values 0 or 1
- parent_features: bfloat16 [16384, 1024], P(('hop', 'node')), may hold values from -6 to 6
- child_slot: int32 [32, 32, 32], P(('hop', 'node')), may hold values from 0 to 511
- parent_slot: int32 [32, 32, 32], P(('hop', 'node')), may hold values from 0 to 511
- importance: int32 [32, 32, 32], P(('hop', 'node')), may hold values from 0 to 16, as said below
- board_proj: bfloat16 [512, 1024], replicated, may hold values from -0.25 to 0.25
- board_bias: float32 [1024], replicated, may hold values from -3 to 3
- neigh_weight: bfloat16 [1024, 1024], replicated, may hold values from -0.1875 to 0.1875
- neigh_bias: float32 [1024], replicated, may hold values from -3 to 3
- comb_weight: bfloat16 [2048, 1024], replicated, may hold values from -0.125 to 0.125
- comb_bias: float32 [1024], replicated, may hold values from -3 to 3
- out_grad: bfloat16 [16384, 1024], P(('hop', 'node')), may hold values from -6 to 6
Outputs:
- embedding: bfloat16 [16384, 1024], P(('hop', 'node'))
- child_grad: bfloat16 [16384, 1024], P(('hop', 'node'))
- parent_grad: bfloat16 [16384, 1024], P(('hop', 'node'))
- board_proj_grad: float32 [512, 1024], replicated
- board_bias_grad: float32 [1024], replicated
- neigh_weight_grad: float32 [1024, 1024], replicated
- neigh_bias_grad: float32 [1024], replicated
- comb_weight_grad: float32 [2048, 1024], replicated
- comb_bias_grad: float32 [1024], replicated
Inputs may be any that keep to these rules, and one draw needn't show every extreme that they name: For receiver r and sender s, importance[r, s, k] is positive for k below a count c(r, s) and 0 from there on; c(r, s) <= 32, and in every draw one receiver has c = 32 from every sender.
All inputs are finite; a program needn't handle non-finite values. No bound on the sum of `child_type` on one device may be relied on, other than what follows from the above.
Results may differ from a plain program's by a relative error of at most 0.0069.
Values may be sent and summed in bfloat16 or wider, within the bound.
A program may use at most 128 MiB of HBM per device.

v0:
```python
import jax
import jax.numpy as jnp
from jax import lax
from jax.sharding import PartitionSpec as P

epsilon = 1e-06


def outer_sum(left, right):
    return lax.dot_general(
        left, right, (((0,), (0,)), ((), ())), preferred_element_type=jnp.float32
    )


def times_transposed(left, right):
    return lax.dot_general(
        left, right, (((1,), (1,)), ((), ())), preferred_element_type=jnp.float32
    )


def silu_slope(value):
    sigma = jax.nn.sigmoid(value)
    return sigma * (1.0 + value * (1.0 - sigma))


def send_rows(buffer):
    return lax.all_to_all(buffer, ("hop", "node"), split_axis=0, concat_axis=0, tiled=True)


def send_grads(buffer):
    return lax.all_to_all(buffer, ("hop", "node"), split_axis=0, concat_axis=0, tiled=True)


def sum_gradients(parts):
    return lax.psum((parts[0], parts[1], parts[2], parts[3], parts[4], parts[5]), ("hop", "node"))


def body(
    child_features,
    child_type,
    parent_features,
    child_slot,
    parent_slot,
    importance,
    board_proj,
    board_bias,
    neigh_weight,
    neigh_bias,
    comb_weight,
    comb_bias,
    out_grad,
):
    width_board = board_proj.shape[0]
    feat_width = child_features.shape[1]
    child_count = child_features.shape[0]
    parent_count = parent_features.shape[0]
    hidden_width = neigh_weight.shape[1]
    senders = child_slot.shape[1]
    capacity = child_slot.shape[2]
    board = (child_type == 1)[:, None]
    left_part = child_features[:, :width_board]
    board_pre = jnp.dot(left_part, board_proj, preferred_element_type=jnp.float32) + board_bias
    child_in = jnp.where(board, board_pre.astype(jnp.bfloat16), child_features)
    neigh_pre = jnp.dot(child_in, neigh_weight, preferred_element_type=jnp.float32) + neigh_bias
    neigh = jax.nn.silu(neigh_pre).astype(jnp.bfloat16)
    child_rows = child_slot.reshape(-1)
    outgoing = jnp.take(neigh, child_rows, axis=0).reshape(senders, capacity, hidden_width)
    incoming = send_rows(outgoing).reshape(senders * capacity, hidden_width)
    weights = importance.reshape(-1).astype(jnp.float32)
    targets = parent_slot.reshape(-1)
    matches = targets[None, :] == jnp.arange(parent_count, dtype=jnp.int32)[:, None]
    weighted = jnp.where(matches, weights[None, :], 0.0)
    total = jnp.maximum(jnp.sum(weighted, axis=1), 1.0)
    sums = jnp.dot(weighted.astype(jnp.bfloat16), incoming, preferred_element_type=jnp.float32)
    agg = sums / total[:, None]
    cat = jnp.concatenate([parent_features, agg.astype(jnp.bfloat16)], axis=1)
    comb_pre = jnp.dot(cat, comb_weight, preferred_element_type=jnp.float32) + comb_bias
    hidden_z = jax.nn.silu(comb_pre)
    inverse = lax.rsqrt(jnp.sum(hidden_z * hidden_z, axis=1, keepdims=True) + epsilon)
    normed = hidden_z * inverse
    embedding = normed.astype(jnp.bfloat16)
    grad_y = out_grad.astype(jnp.float32)
    grad_z = inverse * (grad_y - normed * jnp.sum(normed * grad_y, axis=1, keepdims=True))
    grad_comb = (grad_z * silu_slope(comb_pre)).astype(jnp.bfloat16)
    comb_weight_grad = outer_sum(cat, grad_comb)
    comb_bias_grad = jnp.sum(grad_comb.astype(jnp.float32), axis=0)
    grad_cat = times_transposed(grad_comb, comb_weight)
    parent_grad = grad_cat[:, :feat_width].astype(jnp.bfloat16)
    grad_scaled = grad_cat[:, feat_width:] / total[:, None]
    grad_edges = (jnp.take(grad_scaled, targets, axis=0) * weights[:, None]).astype(jnp.bfloat16)
    returned = send_grads(grad_edges.reshape(senders, capacity, hidden_width))
    grad_neigh = jax.ops.segment_sum(
        returned.reshape(senders * capacity, hidden_width).astype(jnp.float32),
        child_rows,
        num_segments=child_count,
    )
    grad_npre = (grad_neigh * silu_slope(neigh_pre)).astype(jnp.bfloat16)
    neigh_weight_grad = outer_sum(child_in, grad_npre)
    neigh_bias_grad = jnp.sum(grad_npre.astype(jnp.float32), axis=0)
    grad_in = times_transposed(grad_npre, neigh_weight)
    grad_board = jnp.where(board, grad_in, 0.0).astype(jnp.bfloat16)
    board_proj_grad = outer_sum(left_part, grad_board)
    board_bias_grad = jnp.sum(grad_board.astype(jnp.float32), axis=0)
    grad_left = times_transposed(grad_board, board_proj)
    padding = jnp.zeros((child_count, feat_width - width_board), jnp.float32)
    board_rows = jnp.concatenate([grad_left, padding], axis=1)
    child_grad = jnp.where(board, board_rows, grad_in).astype(jnp.bfloat16)
    summed = sum_gradients(
        (
            board_proj_grad,
            board_bias_grad,
            neigh_weight_grad,
            neigh_bias_grad,
            comb_weight_grad,
            comb_bias_grad,
        )
    )
    return (
        embedding,
        child_grad,
        parent_grad,
        summed[0],
        summed[1],
        summed[2],
        summed[3],
        summed[4],
        summed[5],
    )


def solution(mesh):
    in_specs = (
        P(("hop", "node"), None),
        P(("hop", "node")),
        P(("hop", "node"), None),
        P(("hop", "node"), None, None),
        P(("hop", "node"), None, None),
        P(("hop", "node"), None, None),
        P(),
        P(),
        P(),
        P(),
        P(),
        P(),
        P(("hop", "node"), None),
    )
    out_specs = (
        P(("hop", "node"), None),
        P(("hop", "node"), None),
        P(("hop", "node"), None),
        P(),
        P(),
        P(),
        P(),
        P(),
        P(),
    )
    return jax.shard_map(body, mesh=mesh, in_specs=in_specs, out_specs=out_specs, check_vma=False)
```

profile of v0, /device:TPU:0, one launch (start us, length us, event | category | flops | bytes accessed | tf_op | source)
XLA Modules:
  0.0 455.3 jit_solution(8756432768272491844)
XLA Ops:
  7.2 0.9 reshape.148
  9.6 2.4 fusion.7
  12.1 2.7 multiply_convert_fusion.2
  14.8 5.3 %gather_fusion = bf16[1024,1024]{1,0:T(8,128)(2,1)} fusion(bf16[512,1024]{1,0:T(8,128)(2,1)S(1)} %get-tuple-element.33, s32[1024]{0:T(1024)S(1)} %broadcast_clamp_fusion.1), kind=kCustom, calls=%fused_computation | custom fusion | bytes 4198400 | tf_op jit(solution)/shard_map/jit(_take)/gather | solution.py:67
  20.1 3.2 broadcast_select_fusion
  23.3 7.4 %all-to-all-start = ((bf16[32,32,1024]{2,1,0:T(8,128)(2,1)}), bf16[32,32,1024]{2,1,0:T(8,128)(2,1)}, u32[]{:S(2)}, u32[]{:S(2)}) async-start(bf16[32,32,1024]{2,1,0:T(8,128)(2,1)} %broadcast_select_fusion), calls=%async_computation | async-start | bytes 4194304 | tf_op jit(solution)/shard_map/all_to_all | solution.py:27
  31.3 48.3 %all-to-all-done = bf16[32,32,1024]{2,1,0:T(8,128)(2,1)} async-done(((bf16[32,32,1024]{2,1,0:T(8,128)(2,1)}), bf16[32,32,1024]{2,1,0:T(8,128)(2,1)}, u32[]{:S(2)}, u32[]{:S(2)}) %all-to-all-start) | async-done | bytes 2097184 | tf_op jit(solution)/shard_map/all_to_all | solution.py:27
  79.6 3.0 divide_convert_fusion
  82.8 2.8 multiply_reduce_fusion
  86.4 2.2 convert_reduce_fusion
  88.6 2.4 fusion.20
  91.0 1.9 copy-done.3
  92.9 1.6 slice_divide_fusion
  94.5 7.9 %gather_fusion.1 = f32[1024,1024]{1,0:T(8,128)} fusion(f32[512,1024]{1,0:T(8,128)} %slice_divide_fusion, s32[1024]{0:T(1024)S(1)} %broadcast_clamp_fusion), kind=kCustom, calls=%fused_computation.1 | custom fusion | bytes 8392704 | tf_op jit(solution)/shard_map/jit(_take)/gather | solution.py:90
  102.4 3.9 multiply_convert_fusion
  106.4 4.1 all-to-all-start.1
  110.6 7.3 %fusion.8 = f32[2048,1024]{1,0:T(8,128)} fusion(bf16[512,1024]{1,0:T(8,128)(2,1)S(1)} %get-tuple-element.25, bf16[512,1024]{1,0:T(8,128)(2,1)} %copy-done.15, bf16[512,1024]{1,0:T(8,128)(2,1)} %param.15), kind=kOutput, calls=%fused_computation.35 | convolution fusion | flops 2151677952 | bytes 11534336 | tf_op jit(solution)/shard_map/dot_general | solution.py:10
  118.0 41.4 %all-to-all-done.1 = bf16[32,32,1024]{2,1,0:T(8,128)(2,1)} async-done(((bf16[32,32,1024]{2,1,0:T(8,128)(2,1)}), bf16[32,32,1024]{2,1,0:T(8,128)(2,1)}, u32[]{:S(2)}, u32[]{:S(2)}) %all-to-all-start.1) | async-done | bytes 2097184 | tf_op jit(solution)/shard_map/all_to_all | solution.py:31
  159.4 11.1 %scatter_custom_fusion = f32[512,1024]{1,0:T(8,128)} fusion(s32[1024]{0:T(1024)S(1)} %reshape.170, bf16[1024,1024]{1,0:T(8,128)(2,1)} %bitcast.10, f32[]{:T(128)} %constant.21.clone.1), kind=kCustom, calls=%fused_computation.3 | custom fusion | flops 2097152 | bytes 4194308 | tf_op jit(solution)/shard_map/scatter-add | solution.py:92
  170.5 3.1 convert_reduce_fusion.1
  173.5 2.3 convert_reduce_fusion.2
  175.8 3.3 fusion.22
  179.1 2.1 convolution_bitcast_fusion
  181.2 2.7 slice.25
  183.9 40.1 %all-reduce.1 = (f32[1024]{0:T(1024)}, f32[1024]{0:T(1024)}, f32[1024]{0:T(1024)}) all-reduce(f32[1024]{0:T(1024)S(1)} %get-tuple-element.28, f32[1024]{0:T(1024)S(1)} %get-tuple-element.26, f32[1024]{0:T(1024)S(1)} %get-tuple-element.24), channel_id=1, replica_groups=mesh['hop'=4,'node'=8] {'hop','node'}, use_global_device_ids=true, to_apply=%region_6.7 | all-reduce | flops 3072 | bytes 24576 | tf_op jit(solution)/shard_map/psum | solution.py:35
  224.0 2.1 fusion.21
  226.1 1.3 select_convert_fusion.1
  227.4 208.7 %all-reduce.5.cloned.1.call-done = (f32[512,1024]{0,1:T(8,128)}, f32[1024,1024]{1,0:T(8,128)}, f32[2048,1024]{1,0:T(8,128)}) async-done(((f32[512,1024]{0,1:T(8,128)}, f32[1024,1024]{1,0:T(8,128)}, f32[2048,1024]{1,0:T(8,128)}), (f32[512,1024]{0,1:T(8,128)}, f32[1024,1024]{1,0:T(8,128)}, f32[2048,1024]{1,0:T(8,128)})) %all-reduce.5.cloned.1.call-update) | async-done | bytes 14680080 | tf_op jit(solution)/shard_map/psum | solution.py:35
  436.1 2.9 copy.22
  439.0 5.1 %copy.26 = f32[1024,1024]{1,0:T(8,128)} copy(f32[1024,1024]{1,0:T(8,128)} %get-tuple-element.43) | data formatting | bytes 8388608
  444.0 1.1 copy-done.1
  445.1 3.4 copy.27
  (48 shorter events, 3.1 us)
Async XLA Ops:
  7.2 4.8 %copy-start = (bf16[1024,1024]{1,0:T(8,128)(2,1)S(1)}, bf16[1024,1024]{1,0:T(8,128)(2,1)}, u32[]{:S(2)}) copy-start(bf16[1024,1024]{1,0:T(8,128)(2,1)} %param.21) | copy-start | bytes 6291460
  9.6 2.5 copy-start.12
  12.0 2.8 copy-start.4
  23.3 7.4 %copy-start.8 = (s32[1,32,32]{2,1,0:T(8,128)S(1)}, s32[1,32,32]{2,1,0:T(8,128)}, u32[]{:S(2)}) copy-start(s32[1,32,32]{2,1,0:T(8,128)} %param.17) | copy-start | bytes 12292
  23.3 7.6 %copy-start.10 = (s32[1,32,32]{2,1,0:T(8,128)S(1)}, s32[1,32,32]{2,1,0:T(8,128)}, u32[]{:S(2)}) copy-start(s32[1,32,32]{2,1,0:T(8,128)} %param.18) | copy-start | bytes 12292
  23.3 56.3 %all-to-all-start = ((bf16[32,32,1024]{2,1,0:T(8,128)(2,1)}), bf16[32,32,1024]{2,1,0:T(8,128)(2,1)}, u32[]{:S(2)}, u32[]{:S(2)}) async-start(bf16[32,32,1024]{2,1,0:T(8,128)(2,1)} %broadcast_select_fusion), calls=%async_computation | async-start | bytes 4194304 | tf_op jit(solution)/shard_map/all_to_all | solution.py:27
  79.6 3.0 copy-start.11
  79.6 3.0 copy-start.13
  79.6 3.1 copy-start.14
  82.8 2.8 copy-start.15
  82.8 2.8 copy-start.2
  91.0 2.0 copy-start.3
  106.4 4.2 copy-start.9
  106.4 53.0 %all-to-all-start.1 = ((bf16[32,32,1024]{2,1,0:T(8,128)(2,1)}), bf16[32,32,1024]{2,1,0:T(8,128)(2,1)}, u32[]{:S(2)}, u32[]{:S(2)}) async-start(bf16[32,32,1024]{2,1,0:T(8,128)(2,1)} %multiply_convert_fusion), calls=%async_computation.1 | async-start | bytes 4194304 | tf_op jit(solution)/shard_map/all_to_all | solution.py:31
  110.5 325.6 %all-reduce.5.cloned.1.call-start = ((), (), s32[]{:S(2)}) async-start(), calls=%async_computation.2 | async-start | bytes 29360128 | tf_op jit(solution)/shard_map/psum | solution.py:35
  173.5 2.3 copy-start.5
  175.8 3.3 copy-start.7
  224.0 2.1 copy-start.6
  438.9 6.2 %copy-start.1 = (f32[2048,1024]{1,0:T(8,128)S(1)}, f32[2048,1024]{1,0:T(8,128)}, u32[]{:S(2)}) copy-start(f32[2048,1024]{1,0:T(8,128)} %get-tuple-element.45) | copy-start | bytes 25165828
Sparse Core Ops, SparseCore 0:
  181.3 254.6 all-reduce.4
where the time goes:
time: 456 us; the launch traced here: 455 us
  waiting for transfers between devices  298 us (65%)
  blocking collectives  40.1 us (9%)
  local copies, waits for them, and re-layouts  31.8 us (7%)
  matrix products  30.4 us (7%)
  other arithmetic  28.9 us (6%)
  between operations  14.3 us (3%)
  starting transfers between devices  11.6 us (3%)
    psum x1, waiting for transfers between devices, sum_gradients(): lax.psum((parts[0], parts[1], parts[2], parts[3], parts[4], parts[5]), ('...  209 us
    all_to_all x1, waiting for transfers between devices, send_rows(): lax.all_to_all(buffer, ('hop', 'node'), split_axis=0, concat_axis=0, tile...  48.3 us
    all_to_all x1, waiting for transfers between devices, send_grads(): lax.all_to_all(buffer, ('hop', 'node'), split_axis=0, concat_axis=0, tile...  41.4 us
    psum x1, blocking collectives, sum_gradients(): lax.psum((parts[0], parts[1], parts[2], parts[3], parts[4], parts[5]), ('...  40.1 us
    unnamed x35, local copies, waits for them, and re-layouts  14.6 us
    dot_general x3, matrix products, outer_sum(): lax.dot_general(left, right, (((0,), (0,)), ((), ())), preferred_element_...  12.7 us
    scatter-add x1, other arithmetic, body(): jax.ops.segment_sum(returned.reshape(senders * capacity, hidden_width).as...  11.1 us
  transfers between devices with their start and end apart: 3, of which 3 were waited for; matrix products, arithmetic and copies ran while one was open for 3% of the time, Pallas kernels for 0%

commit v1 on v0

v1 whole, which is shorter than its diff:
```python
import functools

import jax
import jax.numpy as jnp
from jax import lax
from jax.experimental import pallas as pl
from jax.experimental.pallas import tpu as pltpu
from jax.sharding import PartitionSpec as P

epsilon = 1e-06
MESH = pl.DeviceIdType.MESH
AXES = ("hop", "node")
f32, bf16 = jnp.float32, jnp.bfloat16


def dot(a, b):
    return jnp.dot(a, b, preferred_element_type=f32)


def outer_sum(left, right):
    return lax.dot_general(left, right, (((0,), (0,)), ((), ())), preferred_element_type=f32)


def times_transposed(left, right):
    return lax.dot_general(left, right, (((1,), (1,)), ((), ())), preferred_element_type=f32)


def silu_slope(value):
    sigma = jax.nn.sigmoid(value)
    return sigma * (1.0 + value * (1.0 - sigma))


def each(count, size, step):
    def one(index, carry):
        step(pl.multiple_of(index * size, size))
        return carry

    lax.fori_loop(0, count // size, one, 0)


class Net:
    def __init__(self, n, node):
        self.n, self.node = n, node
        self.me = lax.axis_index("hop") * node + lax.axis_index("node")
        self.bits = [1 << b for b in range(n.bit_length() - 1)]
        self.bit = {b: (self.me // b) % 2 for b in self.bits}

    def partner(self, mask):
        index = 0
        for b in self.bits:
            index = index + ((self.bit[b] + (mask // b) % 2) % 2) * b
        return (index // self.node, index % self.node), index


class Sems:
    def __init__(self, send, recv):
        self.send, self.recv, self.used = send, recv, 0

    def copy(self, src, dst, where):
        at = self.used
        self.used += 1
        made = pltpu.make_async_remote_copy(
            src_ref=src, dst_ref=dst, send_sem=self.send.at[at], recv_sem=self.recv.at[at],
            device_id=where, device_id_type=MESH,
        )
        made.start()
        return made


def reduce_stream(net, sems, grad, landing, full, first, rows, stages):
    off, length, land = first, rows, first
    trail = []
    for at_stage, bits in enumerate(stages):
        ways = 1 << len(bits)
        part = length // ways
        result = full if at_stage == len(stages) - 1 else grad
        mine = sum(net.bit[b] * (1 << i) for i, b in enumerate(bits))
        sent = []
        for c in range(1, ways):
            mask = sum(b for i, b in enumerate(bits) if (c >> i) & 1)
            theirs = sum(((net.bit[b] + ((c >> i) & 1)) % 2) * (1 << i) for i, b in enumerate(bits))
            src = grad.at[pl.ds(pl.multiple_of(off + theirs * part, 16), part)]
            dst = landing.at[pl.ds(land + (c - 1) * part, part)]
            sent.append(sems.copy(src, dst, net.partner(mask)[0]))
        yield
        for made in sent:
            made.wait()
        keep = off + mine * part
        block = min(part, 64)

        def add(r):
            at = pl.ds(pl.multiple_of(keep + r, 16), block)
            total = grad[at, :].astype(f32)
            for c in range(1, ways):
                total = total + landing[pl.ds(pl.multiple_of(land + (c - 1) * part + r, 16), block), :].astype(f32)
            result[at, :] = total.astype(bf16)

        each(part, block, add)
        trail.append((bits, off, length))
        off, length, land = keep, part, land + (ways - 1) * part
    for bits, whole, size in reversed(trail):
        at = pl.ds(pl.multiple_of(off, 16), length)
        sent = []
        for c in range(1, 1 << len(bits)):
            mask = sum(b for i, b in enumerate(bits) if (c >> i) & 1)
            sent.append(sems.copy(full.at[at], full.at[at], net.partner(mask)[0]))
        yield
        for made in sent:
            made.wait()
        off, length = whole, size


def bias_stream(net, sems, total, landing):
    for i, b in enumerate(net.bits):
        made = sems.copy(total, landing.at[i], net.partner(b)[0])
        yield
        made.wait()
        total[...] = total[...] + landing[i]


def kernel(
    n, node,
    ct, cs, ps, im, bb, nb, cb, cf_h, pf_h, bp_h, nw_h, cw_h, og_h,
    emb_h, cgr_h, pgr_h, gc_h, gn_h, gb_h, bias_h,
    cf, pf, bp, nw, cw, og,
    mask, ci, slope, ng, pick, pick_t, spread, spread_t, inv,
    out_f, in_f, out_b, in_b,
    comb, agg, agg_t, pf_t, ci_t, cf_t, gcomb, gnp, emb,
    gc, rc, gc_sum, gt, rt, gt_sum, bias_c, bias_t, land_c, land_t,
    in_sem, out_sem, a_send, a_recv, r_send, r_recv,
):
    pgr, cgr, gbd = ng, pf, og
    net = Net(n, node)
    sems = Sems(r_send, r_recv)
    me = net.me
    senders, cap = cs.shape
    edges = senders * cap
    children, feat = cf.shape
    parents = pf.shape[0]
    board = bp.shape[0]
    hidden = nw.shape[1]
    half = hidden // 2

    barrier = pltpu.get_barrier_semaphore()

    def greet(i, carry):
        pl.semaphore_signal(barrier, inc=1, device_id=net.partner(i)[0], device_id_type=MESH)
        return carry

    lax.fori_loop(1, n, greet, 0)

    loads = {}
    for i, (name, src, dst) in enumerate(
        [("cf", cf_h, cf), ("bp", bp_h, bp), ("nw", nw_h, nw), ("pf", pf_h, pf), ("cw", cw_h, cw), ("og", og_h, og)]
    ):
        loads[name] = pltpu.make_async_copy(src, dst, in_sem.at[i])
        loads[name].start()

    wide = 128
    eye = lax.broadcasted_iota(jnp.int32, (wide, wide), 0) == lax.broadcasted_iota(jnp.int32, (wide, wide), 1)
    for q in range(ct.shape[0]):
        row = ct[q : q + 1, :].astype(f32)
        mask[pl.ds(q * wide, wide), :] = jnp.sum(jnp.where(eye, row, 0.0), axis=1, keepdims=True)
    small = lax.broadcasted_iota(jnp.int32, (cap, cap), 0) == lax.broadcasted_iota(jnp.int32, (cap, cap), 1)

    def column(ref, s):
        return jnp.sum(jnp.where(small, ref[pl.ds(s, 1), :].astype(f32), 0.0), axis=1, keepdims=True)

    child_lane = lax.broadcasted_iota(jnp.int32, (cap, children), 1).astype(f32)
    parent_lane = lax.broadcasted_iota(jnp.int32, (cap, parents), 1).astype(f32)

    def make_pick(s, carry):
        hit = column(cs, s) == child_lane
        pick[pl.ds(pl.multiple_of(s * cap, 16), cap), :] = jnp.where(hit, 1.0, 0.0).astype(bf16)
        return carry

    lax.fori_loop(0, senders, make_pick, 0)

    loads["cf"].wait()
    loads["bp"].wait()

    def project(c):
        at = pl.ds(c, 256)
        pre = dot(cf[:, 0:board], bp[:, at]) + bb[:, at]
        ci[:, at] = jnp.where(mask[...] > 0.5, pre.astype(bf16), cf[:, at])

    each(feat, 256, project)
    loads["nw"].wait()

    def transform(c):
        at = pl.ds(c, 256)
        pre = dot(ci[...], nw[:, at]) + nb[:, at]
        slope[:, at] = pre
        ng[:, at] = (pre * jax.nn.sigmoid(pre)).astype(bf16)

    each(hidden, 256, transform)

    a_order = n // 2

    def send_all(out, into, h, which):
        def one(i, carry):
            far = i % 2 == 0
            m = jnp.where(far, n - 1 - i // 2, (i + 1) // 2)
            where, index = net.partner(m)
            pltpu.make_async_remote_copy(
                src_ref=out.at[h, pl.ds(pl.multiple_of(index * cap, 16), cap)],
                dst_ref=into.at[h, pl.ds(pl.multiple_of(me * cap, 16), cap)],
                send_sem=a_send.at[which], recv_sem=a_recv.at[which],
                device_id=where, device_id_type=MESH,
            ).start()
            return carry

        lax.fori_loop(0, n - 1, one, 0)
        own = pl.ds(pl.multiple_of(me * cap, 16), cap)
        into[h, own, :] = out[h, own, :]

    def all_of(out, into, h, which):
        return pltpu.make_async_remote_copy(
            src_ref=out.at[h, pl.ds(0, edges - cap)], dst_ref=into.at[h, pl.ds(0, edges - cap)],
            send_sem=a_send.at[which], recv_sem=a_recv.at[which],
            device_id=net.partner(1)[0], device_id_type=MESH,
        )

    for h in range(2):
        def gather(c):
            out_f[h, :, pl.ds(c, 256)] = dot(pick[...], ng[:, pl.ds(pl.multiple_of(h * half + c, 256), 256)]).astype(bf16)

        each(half, 256, gather)
        if h == 0:
            pl.semaphore_wait(barrier, n - 1)
        send_all(out_f, in_f, h, h)

    def make_spread(s, carry):
        hit = column(ps, s) == parent_lane
        spread[pl.ds(pl.multiple_of(s * cap, 16), cap), :] = jnp.where(hit, column(im, s), 0.0).astype(bf16)
        return carry

    lax.fori_loop(0, senders, make_spread, 0)
    spread_t[...] = spread[...].T
    totals = dot(spread_t[...], jnp.ones((edges, 128), bf16))
    inv[...] = 1.0 / jnp.maximum(totals[:, 0:1], 1.0)
    loads["pf"].wait()
    loads["cw"].wait()
    loads["og"].wait()

    def parent_part(c):
        at = pl.ds(c, 256)
        comb[:, at] = dot(pf[...], cw[0:feat, at]) + cb[:, at]

    each(feat, 256, parent_part)
    pick_t[...] = pick[...].T
    pf_t[...] = pf[...].T
    ci_t[...] = ci[...].T
    cf_t[...] = cf[:, 0:board].T

    def to_slope(r):
        at = pl.ds(r, 32)
        slope[at, :] = silu_slope(slope[at, :])

    each(children, 32, to_slope)

    for h in range(2):
        all_of(out_f, in_f, h, h).wait_recv()

        def aggregate(c):
            sums = dot(spread_t[...], in_f[h, :, pl.ds(c, 256)]) * inv[...]
            agg[:, pl.ds(pl.multiple_of(h * half + c, 256), 256)] = sums.astype(bf16)

        each(half, 256, aggregate)

        def combine(c):
            at = pl.ds(c, 256)
            comb[:, at] += dot(agg[:, h * half : (h + 1) * half], cw[feat + h * half : feat + (h + 1) * half, at])

        each(feat, 256, combine)

    bias_c[...] = jnp.zeros_like(bias_c)

    def normalize(r):
        at = pl.ds(r, 32)
        pre = comb[at, :]
        sigma = jax.nn.sigmoid(pre)
        z = pre * sigma
        inverse = lax.rsqrt(jnp.sum(z * z, axis=1, keepdims=True) + epsilon)
        y = z * inverse
        emb[at, :] = y.astype(bf16)
        gy = og[at, :].astype(f32)
        gz = inverse * (gy - y * jnp.sum(y * gy, axis=1, keepdims=True))
        g = (gz * (sigma * (1.0 + pre * (1.0 - sigma)))).astype(bf16)
        gcomb[at, :] = g
        wide_g = g.astype(f32)
        bias_c[...] += wide_g[0:8] + wide_g[8:16] + wide_g[16:24] + wide_g[24:32]

    each(parents, 32, normalize)

    for h in range(2):
        def back(c):
            at = pl.ds(pl.multiple_of(feat + h * half + c, 256), 256)
            scaled = (times_transposed(gcomb[...], cw[at, :]) * inv[...]).astype(bf16)
            out_b[h, :, pl.ds(c, 256)] = dot(spread[...], scaled).astype(bf16)

        each(half, 256, back)
        send_all(out_b, in_b, h, 2 + h)

    stores = []

    def store(src, dst):
        made = pltpu.make_async_copy(src, dst, out_sem.at[len(stores)])
        made.start()
        stores.append(made)

    store(emb, emb_h)
    agg_t[...] = agg[...].T

    def comb_grad(c):
        at = pl.ds(c, 256)
        gc[0:feat, at] = dot(pf_t[...], gcomb[:, at]).astype(bf16)
        gc[feat : feat + hidden, at] = dot(agg_t[...], gcomb[:, at]).astype(bf16)

    each(feat, 256, comb_grad)

    x_first = [[1], [2], [4], [8], [16]]
    y_first = [[1], [4], [2], [8], [16]]
    streams = [
        reduce_stream(net, sems, gc, rc, gc_sum, 512 * i, 512, y_first if i % 2 else x_first) for i in range(gc.shape[0] // 512)
    ]
    biases = [bias_stream(net, sems, bias_c, land_c)]

    def turn(active):
        for stream in list(active):
            if next(stream, "end") == "end":
                active.remove(stream)

    turn(streams)
    turn(biases)

    def parent_back(c):
        pgr[:, pl.ds(c, 256)] = times_transposed(gcomb[...], cw[pl.ds(c, 256), :]).astype(bf16)

    each(feat, 256, parent_back)
    store(pgr, pgr_h)
    for _ in range(5):
        turn(streams)
        turn(biases)

    bias_t[...] = jnp.zeros_like(bias_t)
    for h in range(2):
        all_of(out_b, in_b, h, 2 + h).wait_recv()

        def child_back(c):
            at = pl.ds(pl.multiple_of(h * half + c, 256), 256)
            grown = dot(pick_t[...], in_b[h, :, pl.ds(c, 256)])
            g = (grown * slope[:, at]).astype(bf16)
            gnp[:, at] = g
            bias_t[0:1, at] = jnp.sum(g.astype(f32), axis=0, keepdims=True)
            gt[pl.ds(h * feat, feat), pl.ds(c, 256)] = dot(ci_t[...], g).astype(bf16)

        each(half, 256, child_back)
        more = [
            reduce_stream(net, sems, gt, rt, gt_sum, h * feat + 512 * i, 512, y_first if i % 2 else x_first)
            for i in range(feat // 512)
        ]
        streams += more
        turn(more)

    def into_child(c):
        at = pl.ds(c, 256)
        g_in = times_transposed(gnp[...], nw[at, :])
        is_board = mask[...] > 0.5
        g = jnp.where(is_board, g_in, 0.0).astype(bf16)
        gbd[:, at] = g
        cgr[:, at] = jnp.where(is_board, 0.0, g_in).astype(bf16)
        bias_t[1:2, at] = jnp.sum(g.astype(f32), axis=0, keepdims=True)

    each(feat, 256, into_child)
    for h in range(2):
        def board_grad(c):
            at = pl.ds(pl.multiple_of(h * half + c, 256), 256)
            gt[pl.ds(2 * feat + h * board, board), pl.ds(c, 256)] = dot(cf_t[...], gbd[:, at]).astype(bf16)

        each(half, 256, board_grad)
    more = [
        reduce_stream(net, sems, gt, rt, gt_sum, 2 * feat + board * i, board, y_first if i % 2 else x_first) for i in range(2)
    ]
    streams += more
    turn(more)
    biases.append(bias_stream(net, sems, bias_t, land_t))
    turn(biases)

    def board_back(c):
        at = pl.ds(c, 256)
        left = times_transposed(gbd[...], bp[at, :])
        cgr[:, at] = jnp.where(mask[...] > 0.5, left.astype(bf16), cgr[:, at])

    each(board, 256, board_back)
    store(cgr, cgr_h)
    while streams or biases:
        turn(streams)
        turn(biases)

    store(gc_sum, gc_h)
    for h in range(2):
        store(gt_sum.at[pl.ds(h * feat, feat)], gn_h.at[:, pl.ds(h * half, half)])
        store(gt_sum.at[pl.ds(2 * feat + h * board, board)], gb_h.at[:, pl.ds(h * half, half)])
    store(bias_c, bias_h.at[pl.ds(0, 8)])
    store(bias_t, bias_h.at[pl.ds(8, 8)])
    for which, (out, into) in enumerate([(out_f, in_f), (out_b, in_b)]):
        for h in range(2):
            all_of(out, into, h, 2 * which + h).wait_send()
    for made in stores:
        made.wait()


def fused(n, node, args):
    (child_features, child_type, parent_features, child_slot, parent_slot, importance, board_proj, board_bias,
     neigh_weight, neigh_bias, comb_weight, comb_bias, out_grad) = args
    children, feat = child_features.shape
    parents = parent_features.shape[0]
    board = board_proj.shape[0]
    hidden = neigh_weight.shape[1]
    senders, cap = child_slot.shape[1:]
    edges = senders * cap
    anywhere = pl.BlockSpec(memory_space=pl.ANY)
    vmem = pl.BlockSpec(memory_space=pltpu.VMEM)

    def like(x):
        return pltpu.VMEM(x.shape, x.dtype)

    half = hidden // 2
    steps = n.bit_length() - 1
    grads = pltpu.VMEM((feat + hidden, feat), bf16)
    tail = pltpu.VMEM((2 * feat + 2 * board, half), bf16)
    messages = pltpu.VMEM((2, edges, half), bf16)
    row = pltpu.VMEM((8, feat), f32)
    rows = pltpu.VMEM((steps, 8, feat), f32)
    copies = 10 * steps * 2 + 2 * steps
    out_shape = (
        jax.ShapeDtypeStruct((parents, feat), bf16),
        jax.ShapeDtypeStruct((children, feat), bf16),
        jax.ShapeDtypeStruct((parents, feat), bf16),
        jax.ShapeDtypeStruct((feat + hidden, feat), bf16),
        jax.ShapeDtypeStruct((feat, hidden), bf16),
        jax.ShapeDtypeStruct((board, feat), bf16),
        jax.ShapeDtypeStruct((16, feat), f32),
    )
    result = pl.pallas_call(
        functools.partial(kernel, n, node),
        out_shape=out_shape,
        in_specs=[vmem] * 7 + [anywhere] * 6,
        out_specs=[anywhere] * 7,
        scratch_shapes=[
            like(child_features), like(parent_features), like(board_proj), like(neigh_weight), like(comb_weight), like(out_grad),
            pltpu.VMEM((children, 1), f32),
            pltpu.VMEM((children, feat), bf16),
            pltpu.VMEM((children, hidden), f32),
            pltpu.VMEM((children, hidden), bf16),
            pltpu.VMEM((edges, children), bf16),
            pltpu.VMEM((children, edges), bf16),
            pltpu.VMEM((edges, parents), bf16),
            pltpu.VMEM((parents, edges), bf16),
            pltpu.VMEM((parents, 1), f32),
            messages, messages, messages, messages,
            pltpu.VMEM((parents, feat), f32),
            pltpu.VMEM((parents, hidden), bf16),
            pltpu.VMEM((hidden, parents), bf16),
            pltpu.VMEM((feat, parents), bf16),
            pltpu.VMEM((feat, children), bf16),
            pltpu.VMEM((board, children), bf16),
            pltpu.VMEM((parents, feat), bf16),
            pltpu.VMEM((children, hidden), bf16),
            pltpu.VMEM((parents, feat), bf16),
            grads, grads, grads, tail, tail, tail, row, row, rows, rows,
            pltpu.SemaphoreType.DMA((6,)),
            pltpu.SemaphoreType.DMA((10,)),
            pltpu.SemaphoreType.DMA((4,)),
            pltpu.SemaphoreType.DMA((4,)),
            pltpu.SemaphoreType.DMA((copies,)),
            pltpu.SemaphoreType.DMA((copies,)),
        ],
        compiler_params=pltpu.CompilerParams(
            collective_id=0, has_side_effects=True, vmem_limit_bytes=60 << 20
        ),
    )(
        child_type.reshape(-1, 128), child_slot[0], parent_slot[0], importance[0],
        board_bias[None], neigh_bias[None], comb_bias[None],
        child_features, parent_features, board_proj, neigh_weight, comb_weight, out_grad,
    )
    embedding, child_grad, parent_grad, comb_sum, neigh_sum, board_sum, biases = result
    return (
        embedding, child_grad, parent_grad,
        board_sum.astype(f32), biases[9], neigh_sum.astype(f32), biases[8], comb_sum.astype(f32), jnp.sum(biases[0:8], axis=0),
    )


def send(buffer):
    return lax.all_to_all(buffer, AXES, split_axis=0, concat_axis=0, tiled=True)


def plain(args):
    (child_features, child_type, parent_features, child_slot, parent_slot, importance, board_proj, board_bias,
     neigh_weight, neigh_bias, comb_weight, comb_bias, out_grad) = args
    width_board = board_proj.shape[0]
    child_count, feat_width = child_features.shape
    parent_count = parent_features.shape[0]
    hidden_width = neigh_weight.shape[1]
    senders, capacity = child_slot.shape[1:]
    board = (child_type == 1)[:, None]
    left_part = child_features[:, :width_board]
    board_pre = dot(left_part, board_proj) + board_bias
    child_in = jnp.where(board, board_pre.astype(bf16), child_features)
    neigh_pre = dot(child_in, neigh_weight) + neigh_bias
    neigh = jax.nn.silu(neigh_pre).astype(bf16)
    child_rows = child_slot.reshape(-1)
    outgoing = jnp.take(neigh, child_rows, axis=0).reshape(senders, capacity, hidden_width)
    incoming = send(outgoing).reshape(senders * capacity, hidden_width)
    weights = importance.reshape(-1).astype(f32)
    targets = parent_slot.reshape(-1)
    matches = targets[None, :] == jnp.arange(parent_count, dtype=jnp.int32)[:, None]
    weighted = jnp.where(matches, weights[None, :], 0.0)
    total = jnp.maximum(jnp.sum(weighted, axis=1), 1.0)
    agg = dot(weighted.astype(bf16), incoming) / total[:, None]
    cat = jnp.concatenate([parent_features, agg.astype(bf16)], axis=1)
    comb_pre = dot(cat, comb_weight) + comb_bias
    hidden_z = jax.nn.silu(comb_pre)
    inverse = lax.rsqrt(jnp.sum(hidden_z * hidden_z, axis=1, keepdims=True) + epsilon)
    normed = hidden_z * inverse
    grad_y = out_grad.astype(f32)
    grad_z = inverse * (grad_y - normed * jnp.sum(normed * grad_y, axis=1, keepdims=True))
    grad_comb = (grad_z * silu_slope(comb_pre)).astype(bf16)
    grad_cat = times_transposed(grad_comb, comb_weight)
    grad_scaled = grad_cat[:, feat_width:] / total[:, None]
    grad_edges = (jnp.take(grad_scaled, targets, axis=0) * weights[:, None]).astype(bf16)
    returned = send(grad_edges.reshape(senders, capacity, hidden_width))
    grad_neigh = jax.ops.segment_sum(
        returned.reshape(senders * capacity, hidden_width).astype(f32), child_rows, num_segments=child_count
    )
    grad_npre = (grad_neigh * silu_slope(neigh_pre)).astype(bf16)
    grad_in = times_transposed(grad_npre, neigh_weight)
    grad_board = jnp.where(board, grad_in, 0.0).astype(bf16)
    grad_left = times_transposed(grad_board, board_proj)
    padding = jnp.zeros((child_count, feat_width - width_board), f32)
    child_grad = jnp.where(board, jnp.concatenate([grad_left, padding], axis=1), grad_in).astype(bf16)
    summed = lax.psum(
        (
            outer_sum(left_part, grad_board), jnp.sum(grad_board.astype(f32), axis=0),
            outer_sum(child_in, grad_npre), jnp.sum(grad_npre.astype(f32), axis=0),
            outer_sum(cat, grad_comb), jnp.sum(grad_comb.astype(f32), axis=0),
        ),
        AXES,
    )
    return (normed.astype(bf16), child_grad, grad_cat[:, :feat_width].astype(bf16)) + tuple(summed)


def solution(mesh):
    hop, node = mesh.shape["hop"], mesh.shape["node"]
    n = hop * node

    def body(*args):
        cap = args[3].shape[2]
        if n == 32 and node == 8 and cap % 16 == 0:
            return fused(n, node, args)
        return plain(args)

    rows, cube = P(AXES, None), P(AXES, None, None)
    in_specs = (rows, P(AXES), rows, cube, cube, cube, P(), P(), P(), P(), P(), P(), rows)
    out_specs = (rows, rows, rows, P(), P(), P(), P(), P(), P())
    return jax.shard_map(body, mesh=mesh, in_specs=in_specs, out_specs=out_specs, check_vma=False)
```

time: 456 us -> 213 us (0.47)
  waiting for transfers between devices: 298 us -> 0 us
  Pallas kernels: 0 us -> 195 us
  blocking collectives: 40.1 us -> 0 us
  matrix products: 30.4 us -> 0 us
  local copies, waits for them, and re-layouts: 31.8 us -> 4.36 us
  other arithmetic: 28.9 us -> 12.2 us
  between operations: 14.3 us -> 0.66 us
  starting transfers between devices: 11.6 us -> 0 us
    psum x1 -> x0, waiting for transfers between devices: 209 us -> none  [sum_gradients(): lax.psum((parts[0], parts[1], parts[2], parts[3], parts[4], parts[5]), ('...]
    pallas_call x0 -> x1, Pallas kernels: none -> 195 us  [fused(): pl.pallas_call(functools.partial(kernel, n, node), out_shape=out_shape, i...]
    all_to_all x2 -> x0, waiting for transfers between devices: 89.7 us -> none  [the longest x1 48.3 us: send_rows(): lax.all_to_all(buffer, ('hop', 'node'), split_axis=0, concat_axis=0, tile...]
    psum x1 -> x0, blocking collectives: 40.1 us -> none  [sum_gradients(): lax.psum((parts[0], parts[1], parts[2], parts[3], parts[4], parts[5]), ('...]
    dot_general x10 -> x0, matrix products: 30.4 us -> none  [the longest x3 12.7 us: outer_sum(): lax.dot_general(left, right, (((0,), (0,)), ((), ())), preferred_element_...]
    gather x2 -> x0, local copies, waits for them, and re-layouts: 13.3 us -> none  [the longest x1 7.92 us: body(): jnp.take(grad_scaled, targets, axis=0) * weights[:, None]]
    unnamed x35 -> x13, local copies, waits for them, and re-layouts: 14.6 us -> 2.93 us
    all_to_all x2 -> x0, starting transfers between devices: 11.6 us -> none  [the longest x1 7.43 us: send_rows(): lax.all_to_all(buffer, ('hop', 'node'), split_axis=0, concat_axis=0, tile...]
  transfers between devices with their start and end apart: 3 -> 0, of which waited for: 3 -> 0; matrix products, arithmetic and copies ran while one was open for 3% -> 0% of each run, Pallas kernels for 0% -> 0%
where the time goes in v1:
time: 213 us; the launch traced here: 212 us
  Pallas kernels  195 us (92%)
  other arithmetic  12.2 us (6%)
  local copies, waits for them, and re-layouts  4.36 us (2%)
    pallas_call x1, Pallas kernels, fused(): pl.pallas_call(functools.partial(kernel, n, node), out_shape=out_shape, i...  195 us
    convert_element_type x1, other arithmetic, fused(): comb_sum.astype(f32)  6.78 us

profile of v1, /device:TPU:0, one launch (start us, length us, event | category | flops | bytes accessed | tf_op | source)
XLA Modules:
  0.0 212.3 jit_solution(16328940034441121833)
XLA Ops:
  0.6 195.1 %shard_map.196 = (bf16[512,1024]{1,0:T(8,128)(2,1)}, bf16[512,1024]{1,0:T(8,128)(2,1)}, bf16[512,1024]{1,0:T(8,128)(2,1)}, bf16[2048,1024]{1,0:T(8,128)(2,1)}, b...) custom-call(s32[4,128]{1,0:T(4,128)} %bitcast.17, s32[32,32]{1,0:T(8,128)} %bitcast.9, ...), custom_call_target="tpu_custom_call" | custom-call | tf_op jit(solution)/shard_map/pallas_call | solution.py:446
  195.8 1.4 fusion
  197.2 1.4 slice_reduce_fusion
  198.5 0.0 copy-start
  198.5 6.8 %convert_element_type.11 = f32[2048,1024]{1,0:T(8,128)} convert(bf16[2048,1024]{1,0:T(8,128)(2,1)} %get-tuple-element.22) | non-fusion elementwise | flops 2097152 | bytes 12582912 | tf_op jit(solution)/shard_map/convert_element_type | solution.py:491
  205.3 0.0 copy-start.1
  205.3 0.0 copy-done
  205.3 0.0 copy-start.4
  205.3 2.5 %convert_element_type.10 = f32[1024,1024]{1,0:T(8,128)} convert(bf16[1024,1024]{1,0:T(8,128)(2,1)S(1)} %copy-done) | non-fusion elementwise | flops 1048576 | bytes 6291456 | tf_op jit(solution)/shard_map/convert_element_type | solution.py:491
  207.8 0.0 copy-start.3
  207.8 0.0 copy-start.2
  207.8 0.0 copy-done.1
  207.8 1.6 convert_element_type.9
  209.4 0.0 copy-done.4
  209.4 1.0 copy.25
  210.4 0.0 copy-done.3
  210.4 1.0 copy.26
  211.3 0.0 copy-done.2
  211.3 1.0 copy.27
Async XLA Ops:
  198.5 6.8 %copy-start = (bf16[1024,1024]{1,0:T(8,128)(2,1)S(1)}, bf16[1024,1024]{1,0:T(8,128)(2,1)}, u32[]{:S(2)}) copy-start(bf16[1024,1024]{1,0:T(8,128)(2,1)} %get-tuple-element.21) | copy-start | bytes 6291460
  205.3 2.5 %copy-start.1 = (bf16[512,1024]{1,0:T(8,128)(2,1)S(1)}, bf16[512,1024]{1,0:T(8,128)(2,1)}, u32[]{:S(2)}) copy-start(bf16[512,1024]{1,0:T(8,128)(2,1)} %get-tuple-element.19) | copy-start | bytes 3145732
  205.3 4.1 %copy-start.4 = (bf16[512,1024]{1,0:T(8,128)(2,1)S(1)}, bf16[512,1024]{1,0:T(8,128)(2,1)}, u32[]{:S(2)}) copy-start(bf16[512,1024]{1,0:T(8,128)(2,1)} %get-tuple-element.34) | copy-start | bytes 3145732
  207.8 2.5 %copy-start.3 = (bf16[512,1024]{1,0:T(8,128)(2,1)S(1)}, bf16[512,1024]{1,0:T(8,128)(2,1)}, u32[]{:S(2)}) copy-start(bf16[512,1024]{1,0:T(8,128)(2,1)} %get-tuple-element.35) | copy-start | bytes 3145732
  207.8 3.5 %copy-start.2 = (bf16[512,1024]{1,0:T(8,128)(2,1)S(1)}, bf16[512,1024]{1,0:T(8,128)(2,1)}, u32[]{:S(2)}) copy-start(bf16[512,1024]{1,0:T(8,128)(2,1)} %get-tuple-element.36) | copy-start | bytes 3145732

commit v2 on v1

--- a/solution.py
+++ b/solution.py
@@ -10,6 +10,18 @@
 epsilon = 1e-06
 MESH = pl.DeviceIdType.MESH
 AXES = ("hop", "node")
+K2_LIMIT = 36
+X_FIRST = [[1], [2], [4], [8], [16]]
+Y_FIRST = [[1], [4], [2], [8], [16]]
+X_DIRECT = [[1], [2], [4], [8, 16]]
+Y_DIRECT = [[1], [4], [2], [8, 16]]
+COMB_ORDERS = [X_FIRST, Y_FIRST] * 4
+TAIL_ORDERS = [X_DIRECT, Y_DIRECT, Y_DIRECT, X_DIRECT, Y_DIRECT, X_DIRECT]
+PLAN = (
+    "S0", "S1", "G0", "c0", "G1", "c0", "c1", "G2", "c0", "c1", "c2", "G3", "BC", "P", "c0", "c1", "c2", "c3", "bc",
+    "A0", "c0", "c1", "c2", "c3", "A1", "BT", "c0", "c1", "c2", "c3", "n0", "n1", "I",
+)
+LATE = ("c0", "c1", "c2", "c3", "bc", "n0", "n1", "bt")
 f32, bf16 = jnp.float32, jnp.bfloat16
 
 
@@ -67,19 +79,18 @@
         return made
 
 
-def reduce_stream(net, sems, grad, landing, full, first, rows, stages):
-    off, length, land = first, rows, first
+def reduce_stream(net, sems, grad, landing, full, own_sem, first, rows, stages):
+    off, length, land = 0, rows, first
     trail = []
-    for at_stage, bits in enumerate(stages):
+    for bits in stages:
         ways = 1 << len(bits)
         part = length // ways
-        result = full if at_stage == len(stages) - 1 else grad
         mine = sum(net.bit[b] * (1 << i) for i, b in enumerate(bits))
         sent = []
         for c in range(1, ways):
             mask = sum(b for i, b in enumerate(bits) if (c >> i) & 1)
             theirs = sum(((net.bit[b] + ((c >> i) & 1)) % 2) * (1 << i) for i, b in enumerate(bits))
-            src = grad.at[pl.ds(pl.multiple_of(off + theirs * part, 16), part)]
+            src = grad.at[pl.ds(pl.multiple_of(first + off + theirs * part, 16), part)]
             dst = landing.at[pl.ds(land + (c - 1) * part, part)]
             sent.append(sems.copy(src, dst, net.partner(mask)[0]))
         yield
@@ -89,25 +100,32 @@
         block = min(part, 64)
 
         def add(r):
-            at = pl.ds(pl.multiple_of(keep + r, 16), block)
+            at = pl.ds(pl.multiple_of(first + keep + r, 16), block)
             total = grad[at, :].astype(f32)
             for c in range(1, ways):
                 total = total + landing[pl.ds(pl.multiple_of(land + (c - 1) * part + r, 16), block), :].astype(f32)
-            result[at, :] = total.astype(bf16)
+            grad[at, :] = total.astype(bf16)
 
         each(part, block, add)
         trail.append((bits, off, length))
         off, length, land = keep, part, land + (ways - 1) * part
+    source = grad.at[pl.ds(pl.multiple_of(first + off, 16), length)]
+    own = pltpu.make_async_copy(source, full.at[pl.ds(pl.multiple_of(off, 16), length)], own_sem)
+    own.start()
     for bits, whole, size in reversed(trail):
-        at = pl.ds(pl.multiple_of(off, 16), length)
+        at = full.at[pl.ds(pl.multiple_of(off, 16), length)]
+        if source is None:
+            source = at
         sent = []
         for c in range(1, 1 << len(bits)):
             mask = sum(b for i, b in enumerate(bits) if (c >> i) & 1)
-            sent.append(sems.copy(full.at[at], full.at[at], net.partner(mask)[0]))
+            sent.append(sems.copy(source, at, net.partner(mask)[0]))
         yield
+        if own is not None:
+            own.wait()
         for made in sent:
             made.wait()
-        off, length = whole, size
+        off, length, source, own = whole, size, None, None
 
 
 def bias_stream(net, sems, total, landing):
@@ -120,16 +138,16 @@
 
 def kernel(
     n, node,
-    ct, cs, ps, im, bb, nb, cb, cf_h, pf_h, bp_h, nw_h, cw_h, og_h,
-    emb_h, cgr_h, pgr_h, gc_h, gn_h, gb_h, bias_h,
-    cf, pf, bp, nw, cw, og,
+    ct_h, cs_h, ps_h, im_h, bb_h, nb_h, cb_h, cf_h, pf_h, bp_h, nw_h, cw_h, og_h,
+    emb_h, cgr_h, pgr_h, c0_h, c1_h, c2_h, c3_h, n0_h, n1_h, bias_h,
+    ct, cs, ps, im, bb, nb, cb, cf, pf, bp, nw, cw, og,
     mask, ci, slope, ng, pick, pick_t, spread, spread_t, inv,
-    out_f, in_f, out_b, in_b,
-    comb, agg, agg_t, pf_t, ci_t, cf_t, gcomb, gnp, emb,
-    gc, rc, gc_sum, gt, rt, gt_sum, bias_c, bias_t, land_c, land_t,
-    in_sem, out_sem, a_send, a_recv, r_send, r_recv,
+    out_f, in_f, in_b,
+    comb, agg, pf_t, left_t,
+    grad, landing, bias_c, bias_t, land_c, land_t,
+    in_sem, out_sem, own_sem, a_send, a_recv, r_send, r_recv,
 ):
-    pgr, cgr, gbd = ng, pf, og
+    pgr, cgr, gbd, agg_t, gnp, out_b, emb, gcomb = ng, pf, og, pick, spread_t, out_f, cf, ci
     net = Net(n, node)
     sems = Sems(r_send, r_recv)
     me = net.me
@@ -151,11 +169,16 @@
 
     loads = {}
     for i, (name, src, dst) in enumerate(
-        [("cf", cf_h, cf), ("bp", bp_h, bp), ("nw", nw_h, nw), ("pf", pf_h, pf), ("cw", cw_h, cw), ("og", og_h, og)]
+        [
+            ("cs", cs_h, cs), ("ct", ct_h, ct), ("bb", bb_h, bb), ("nb", nb_h, nb), ("cf", cf_h, cf), ("bp", bp_h, bp), ("nw", nw_h, nw),
+            ("ps", ps_h, ps), ("im", im_h, im), ("cb", cb_h, cb), ("pf", pf_h, pf), ("cw", cw_h, cw), ("og", og_h, og),
+        ]
     ):
         loads[name] = pltpu.make_async_copy(src, dst, in_sem.at[i])
         loads[name].start()
 
+    for name in ("cs", "ct", "bb", "nb"):
+        loads[name].wait()
     wide = 128
     eye = lax.broadcasted_iota(jnp.int32, (wide, wide), 0) == lax.broadcasted_iota(jnp.int32, (wide, wide), 1)
     for q in range(ct.shape[0]):
@@ -230,6 +253,9 @@
             pl.semaphore_wait(barrier, n - 1)
         send_all(out_f, in_f, h, h)
 
+    for name in ("ps", "im", "cb"):
+        loads[name].wait()
+
     def make_spread(s, carry):
         hit = column(ps, s) == parent_lane
         spread[pl.ds(pl.multiple_of(s * cap, 16), cap), :] = jnp.where(hit, column(im, s), 0.0).astype(bf16)
@@ -250,8 +276,8 @@
     each(feat, 256, parent_part)
     pick_t[...] = pick[...].T
     pf_t[...] = pf[...].T
-    ci_t[...] = ci[...].T
-    cf_t[...] = cf[:, 0:board].T
+    left_t[0:feat, :] = ci[...].T
+    left_t[feat : feat + board, :] = jnp.where(mask[...] > 0.5, cf[:, 0:board], jnp.zeros((), bf16)).T
 
     def to_slope(r):
         at = pl.ds(r, 32)
@@ -293,120 +319,199 @@
 
     each(parents, 32, normalize)
 
-    for h in range(2):
+    stores = []
+
+    def store(src, dst):
+        made = pltpu.make_async_copy(src, dst, out_sem.at[len(stores)])
+        made.start()
+        stores.append(made)
+
+    groups = {}
+    streams = []
+
+    sums = dict(c0=c0_h, c1=c1_h, c2=c2_h, c3=c3_h, n0=n0_h, n1=n1_h)
+
+    def begin(name, first, orders):
+        groups[name] = []
+        for i, stages in enumerate(orders):
+            to = sums[name].at[pl.ds(512 * i, 512)]
+            streams.append(first)
+            groups[name].append(reduce_stream(
+                net, sems, grad, landing, to, own_sem.at[len(streams) - 1], first + 512 * i, 512, stages
+            ))
+        turn(name)
+
+    def turn(name):
+        for stream in list(groups[name]):
+            if next(stream, "end") == "end":
+                groups[name].remove(stream)
+
+    def send_back(h):
         def back(c):
             at = pl.ds(pl.multiple_of(feat + h * half + c, 256), 256)
             scaled = (times_transposed(gcomb[...], cw[at, :]) * inv[...]).astype(bf16)
             out_b[h, :, pl.ds(c, 256)] = dot(spread[...], scaled).astype(bf16)
 
+        all_of(out_f, in_f, h, h).wait_send()
         each(half, 256, back)
         send_all(out_b, in_b, h, 2 + h)
 
-    stores = []
-
-    def store(src, dst):
-        made = pltpu.make_async_copy(src, dst, out_sem.at[len(stores)])
-        made.start()
-        stores.append(made)
-
-    store(emb, emb_h)
-    agg_t[...] = agg[...].T
-
-    def comb_grad(c):
-        at = pl.ds(c, 256)
-        gc[0:feat, at] = dot(pf_t[...], gcomb[:, at]).astype(bf16)
-        gc[feat : feat + hidden, at] = dot(agg_t[...], gcomb[:, at]).astype(bf16)
-
-    each(feat, 256, comb_grad)
-
-    x_first = [[1], [2], [4], [8], [16]]
-    y_first = [[1], [4], [2], [8], [16]]
-    streams = [
-        reduce_stream(net, sems, gc, rc, gc_sum, 512 * i, 512, y_first if i % 2 else x_first) for i in range(gc.shape[0] // 512)
-    ]
-    biases = [bias_stream(net, sems, bias_c, land_c)]
-
-    def turn(active):
-        for stream in list(active):
-            if next(stream, "end") == "end":
-                active.remove(stream)
-
-    turn(streams)
-    turn(biases)
-
-    def parent_back(c):
-        pgr[:, pl.ds(c, 256)] = times_transposed(gcomb[...], cw[pl.ds(c, 256), :]).astype(bf16)
-
-    each(feat, 256, parent_back)
-    store(pgr, pgr_h)
-    for _ in range(5):
-        turn(streams)
-        turn(biases)
-
-    bias_t[...] = jnp.zeros_like(bias_t)
-    for h in range(2):
+    def comb_sum(k):
+        h, part = k // 2, k % 2
+        if k == 1:
+            agg_t[...] = agg[...].T
+        left = agg_t if part else pf_t
+        base = k * feat
+
+        def comb_grad(c):
+            at = pl.ds(pl.multiple_of(h * half + c, 256), 256)
+            grad[pl.ds(base, feat), pl.ds(c, 256)] = dot(left[...], gcomb[:, at]).astype(bf16)
+
+        each(half, 256, comb_grad)
+        begin("c%d" % k, base, COMB_ORDERS[2 * k : 2 * k + 2])
+
+    def parent_out():
+        def parent_back(c):
+            pgr[:, pl.ds(c, 256)] = times_transposed(gcomb[...], cw[pl.ds(c, 256), :]).astype(bf16)
+
+        each(feat, 256, parent_back)
+        store(emb, emb_h)
+        store(pgr, pgr_h)
+
+    def child_sum(h):
         all_of(out_b, in_b, h, 2 + h).wait_recv()
+        first = 4 * feat + h * (feat + board)
 
         def child_back(c):
             at = pl.ds(pl.multiple_of(h * half + c, 256), 256)
             grown = dot(pick_t[...], in_b[h, :, pl.ds(c, 256)])
             g = (grown * slope[:, at]).astype(bf16)
             gnp[:, at] = g
-            bias_t[0:1, at] = jnp.sum(g.astype(f32), axis=0, keepdims=True)
-            gt[pl.ds(h * feat, feat), pl.ds(c, 256)] = dot(ci_t[...], g).astype(bf16)
+            grad[pl.ds(first, feat + board), pl.ds(c, 256)] = dot(left_t[...], g).astype(bf16)
 
         each(half, 256, child_back)
-        more = [
-            reduce_stream(net, sems, gt, rt, gt_sum, h * feat + 512 * i, 512, y_first if i % 2 else x_first)
-            for i in range(feat // 512)
-        ]
-        streams += more
-        turn(more)
-
-    def into_child(c):
-        at = pl.ds(c, 256)
-        g_in = times_transposed(gnp[...], nw[at, :])
-        is_board = mask[...] > 0.5
-        g = jnp.where(is_board, g_in, 0.0).astype(bf16)
-        gbd[:, at] = g
-        cgr[:, at] = jnp.where(is_board, 0.0, g_in).astype(bf16)
-        bias_t[1:2, at] = jnp.sum(g.astype(f32), axis=0, keepdims=True)
-
-    each(feat, 256, into_child)
+        begin("n%d" % h, first, TAIL_ORDERS[3 * h : 3 * h + 3])
+
+    def bias_sum(name, total, landing_rows):
+        groups[name] = [bias_stream(net, sems, total, landing_rows)]
+        turn(name)
+
+    def child_biases():
+        bias_t[...] = jnp.zeros_like(bias_t)
+
+        def sums_of(c):
+            at = pl.ds(c, 256)
+            g = gnp[:, at].astype(f32)
+            bias_t[0:1, at] = jnp.sum(g, axis=0, keepdims=True)
+            bias_t[1:2, at] = jnp.sum(jnp.where(mask[...] > 0.5, g, 0.0), axis=0, keepdims=True)
+
+        each(hidden, 256, sums_of)
+        bias_sum("bt", bias_t, land_t)
+
+    def child_out():
+        def into_child(c):
+            at = pl.ds(c, 256)
+            g_in = times_transposed(gnp[...], nw[at, :])
+            is_board = mask[...] > 0.5
+            gbd[:, at] = jnp.where(is_board, g_in, 0.0).astype(bf16)
+            cgr[:, at] = jnp.where(is_board, 0.0, g_in).astype(bf16)
+
+        each(feat, 256, into_child)
+
+        def board_back(c):
+            at = pl.ds(c, 256)
+            left = times_transposed(gbd[...], bp[at, :])
+            cgr[:, at] = jnp.where(mask[...] > 0.5, left.astype(bf16), cgr[:, at])
+
+        each(board, 256, board_back)
+        store(cgr, cgr_h)
+
+    tasks = {
+        "S0": lambda: send_back(0), "S1": lambda: send_back(1),
+        "G0": lambda: comb_sum(0), "G1": lambda: comb_sum(1), "G2": lambda: comb_sum(2), "G3": lambda: comb_sum(3),
+        "A0": lambda: child_sum(0), "A1": lambda: child_sum(1),
+        "BC": lambda: bias_sum("bc", bias_c, land_c), "BT": child_biases, "P": parent_out, "I": child_out,
+    }
+    for token in PLAN:
+        if token in tasks:
+            tasks[token]()
+        else:
+            turn(token)
+    while any(groups.values()):
+        for name in LATE:
+            turn(name)
+
+    bias_h[0:8, :] = bias_c[...]
+    bias_h[8:16, :] = bias_t[...]
     for h in range(2):
-        def board_grad(c):
-            at = pl.ds(pl.multiple_of(h * half + c, 256), 256)
-            gt[pl.ds(2 * feat + h * board, board), pl.ds(c, 256)] = dot(cf_t[...], gbd[:, at]).astype(bf16)
-
-        each(half, 256, board_grad)
-    more = [
-        reduce_stream(net, sems, gt, rt, gt_sum, 2 * feat + board * i, board, y_first if i % 2 else x_first) for i in range(2)
+        all_of(out_b, in_b, h, 2 + h).wait_send()
+    for made in stores:
+        made.wait()
+
+
+def widen(
+    bias_ref, c0_h, c1_h, c2_h, c3_h, n0_h, n1_h, nw_h, emb_h, cgr_h, pgr_h,
+    comb_o, neigh_o, proj_o, emb_o, cgr_o, pgr_o, comb_b, neigh_b, proj_b,
+    sums, nw, wide, emb, cgr, pgr, sum_sem, nw_sem, row_sem, out_sem,
+):
+    feat = nw.shape[0]
+    board = proj_o.shape[0]
+    half = feat // 2
+    block = 512
+    per = feat // block
+
+    def piece(i):
+        if i < 2 * per:
+            at = pl.ds((i % per) * block, block)
+            return [(c0_h, c1_h)[i // per].at[at], (c2_h, c3_h)[i // per].at[at]]
+        at = pl.ds((i - 2 * per) * block, block)
+        return [n0_h.at[at], n1_h.at[at]]
+
+    chunks = [pl.ds(i * block, block) for i in range(sums.shape[1] // block)]
+    loads = [
+        [pltpu.make_async_copy(src, sums.at[h, at], sum_sem.at[2 * i + h]) for h, src in enumerate(piece(i))]
+        for i, at in enumerate(chunks)
     ]
-    streams += more
-    turn(more)
-    biases.append(bias_stream(net, sems, bias_t, land_t))
-    turn(biases)
-
-    def board_back(c):
-        at = pl.ds(c, 256)
-        left = times_transposed(gbd[...], bp[at, :])
-        cgr[:, at] = jnp.where(mask[...] > 0.5, left.astype(bf16), cgr[:, at])
-
-    each(board, 256, board_back)
-    store(cgr, cgr_h)
-    while streams or biases:
-        turn(streams)
-        turn(biases)
-
-    store(gc_sum, gc_h)
-    for h in range(2):
-        store(gt_sum.at[pl.ds(h * feat, feat)], gn_h.at[:, pl.ds(h * half, half)])
-        store(gt_sum.at[pl.ds(2 * feat + h * board, board)], gb_h.at[:, pl.ds(h * half, half)])
-    store(bias_c, bias_h.at[pl.ds(0, 8)])
-    store(bias_t, bias_h.at[pl.ds(8, 8)])
-    for which, (out, into) in enumerate([(out_f, in_f), (out_b, in_b)]):
-        for h in range(2):
-            all_of(out, into, h, 2 * which + h).wait_send()
+    load_nw = pltpu.make_async_copy(nw_h, nw, nw_sem)
+    rows = [(emb_h, emb, emb_o), (cgr_h, cgr, cgr_o), (pgr_h, pgr, pgr_o)]
+    row_loads = [pltpu.make_async_copy(src, mid, row_sem.at[i]) for i, (src, mid, _) in enumerate(rows)]
+    for made in row_loads + sum(loads, []):
+        made.start()
+    load_nw.start()
+    stores = []
+
+    def store(src, dst):
+        made = pltpu.make_async_copy(src, dst, out_sem.at[len(stores)])
+        made.start()
+        stores.append(made)
+
+    for made, (_, mid, dst) in zip(row_loads, rows):
+        made.wait()
+        store(mid, dst)
+    for i, at in enumerate(chunks):
+        for made in loads[i]:
+            made.wait()
+        if i * block < 3 * feat:
+            for h in range(2):
+                wide[at, h * half : (h + 1) * half] = sums[h, at, :].astype(f32)
+            if i * block < 2 * feat:
+                store(wide.at[at], comb_o.at[at])
+            else:
+                store(wide.at[at], neigh_o.at[pl.ds(i * block - 2 * feat, block)])
+    load_nw.wait()
+    for r in range(0, board, block):
+        at = pl.ds(3 * feat + r, block)
+        wide[at, :] = times_transposed(sums[0, at, :], nw[:, 0:half]) + times_transposed(sums[1, at, :], nw[:, half:])
+        store(wide.at[at], proj_o.at[pl.ds(r, block)])
+    comb_b[...] = jnp.sum(bias_ref[0:8, :], axis=0, keepdims=True)
+    neigh_b[...] = bias_ref[8:9, :]
+    line = jnp.broadcast_to(bias_ref[9:10, :], (16, feat))
+    high = line.astype(bf16)
+    rest = line - high.astype(f32)
+    low = rest.astype(bf16)
+    lowest = (rest - low.astype(f32)).astype(bf16)
+    parts = [times_transposed(x, nw[...]) for x in (high, low, lowest)]
+    proj_b[...] = (parts[0] + (parts[1] + parts[2]))[0:1]
     for made in stores:
         made.wait()
 
@@ -422,33 +527,37 @@
     edges = senders * cap
     anywhere = pl.BlockSpec(memory_space=pl.ANY)
     vmem = pl.BlockSpec(memory_space=pltpu.VMEM)
+    in_hbm = pl.BlockSpec(memory_space=pltpu.HBM)
 
     def like(x):
         return pltpu.VMEM(x.shape, x.dtype)
 
+    small = (
+        child_type.reshape(-1, 128), child_slot[0], parent_slot[0], importance[0],
+        board_bias[None], neigh_bias[None], comb_bias[None],
+    )
     half = hidden // 2
     steps = n.bit_length() - 1
-    grads = pltpu.VMEM((feat + hidden, feat), bf16)
-    tail = pltpu.VMEM((2 * feat + 2 * board, half), bf16)
+    grads = pltpu.VMEM((6 * feat + 2 * board, half), bf16)
     messages = pltpu.VMEM((2, edges, half), bf16)
     row = pltpu.VMEM((8, feat), f32)
     rows = pltpu.VMEM((steps, 8, feat), f32)
-    copies = 10 * steps * 2 + 2 * steps
+    copies = 14 * 14 + 2 * steps
     out_shape = (
         jax.ShapeDtypeStruct((parents, feat), bf16),
         jax.ShapeDtypeStruct((children, feat), bf16),
         jax.ShapeDtypeStruct((parents, feat), bf16),
-        jax.ShapeDtypeStruct((feat + hidden, feat), bf16),
-        jax.ShapeDtypeStruct((feat, hidden), bf16),
-        jax.ShapeDtypeStruct((board, feat), bf16),
+        *[jax.ShapeDtypeStruct((feat, half), bf16)] * 4,
+        *[jax.ShapeDtypeStruct((feat + board, half), bf16)] * 2,
         jax.ShapeDtypeStruct((16, feat), f32),
     )
     result = pl.pallas_call(
         functools.partial(kernel, n, node),
         out_shape=out_shape,
-        in_specs=[vmem] * 7 + [anywhere] * 6,
-        out_specs=[anywhere] * 7,
+        in_specs=[in_hbm] * 13,
+        out_specs=[anywhere] * 9 + [vmem],
         scratch_shapes=[
+            *[like(x) for x in small],
             like(child_features), like(parent_features), like(board_proj), like(neigh_weight), like(comb_weight), like(out_grad),
             pltpu.VMEM((children, 1), f32),
             pltpu.VMEM((children, feat), bf16),
@@ -459,37 +568,48 @@
             pltpu.VMEM((edges, parents), bf16),
             pltpu.VMEM((parents, edges), bf16),
             pltpu.VMEM((parents, 1), f32),
-            messages, messages, messages, messages,
+            messages, messages, messages,
             pltpu.VMEM((parents, feat), f32),
             pltpu.VMEM((parents, hidden), bf16),
-            pltpu.VMEM((hidden, parents), bf16),
             pltpu.VMEM((feat, parents), bf16),
-            pltpu.VMEM((feat, children), bf16),
-            pltpu.VMEM((board, children), bf16),
-            pltpu.VMEM((parents, feat), bf16),
-            pltpu.VMEM((children, hidden), bf16),
-            pltpu.VMEM((parents, feat), bf16),
-            grads, grads, grads, tail, tail, tail, row, row, rows, rows,
-            pltpu.SemaphoreType.DMA((6,)),
-            pltpu.SemaphoreType.DMA((10,)),
+            pltpu.VMEM((feat + board, children), bf16),
+            grads, grads, row, row, rows, rows,
+            pltpu.SemaphoreType.DMA((13,)),
+            pltpu.SemaphoreType.DMA((3,)),
+            pltpu.SemaphoreType.DMA((14,)),
             pltpu.SemaphoreType.DMA((4,)),
             pltpu.SemaphoreType.DMA((4,)),
             pltpu.SemaphoreType.DMA((copies,)),
             pltpu.SemaphoreType.DMA((copies,)),
         ],
         compiler_params=pltpu.CompilerParams(
-            collective_id=0, has_side_effects=True, vmem_limit_bytes=60 << 20
+            collective_id=0, has_side_effects=True, vmem_limit_bytes=46 << 20
         ),
     )(
-        child_type.reshape(-1, 128), child_slot[0], parent_slot[0], importance[0],
-        board_bias[None], neigh_bias[None], comb_bias[None],
+        *[pltpu.with_memory_space_constraint(x, pltpu.HBM) for x in small],
         child_features, parent_features, board_proj, neigh_weight, comb_weight, out_grad,
     )
-    embedding, child_grad, parent_grad, comb_sum, neigh_sum, board_sum, biases = result
-    return (
-        embedding, child_grad, parent_grad,
-        board_sum.astype(f32), biases[9], neigh_sum.astype(f32), biases[8], comb_sum.astype(f32), jnp.sum(biases[0:8], axis=0),
-    )
+    embedding, child_grad, parent_grad = result[:3]
+    row_out = jax.ShapeDtypeStruct((1, feat), f32)
+    total = 3 * feat + board
+    chunks = total // 512
+    comb_g, neigh_g, proj_g, embedding, child_grad, parent_grad, comb_b, neigh_b, proj_b = pl.pallas_call(
+        widen,
+        out_shape=(
+            jax.ShapeDtypeStruct((2 * feat, feat), f32), jax.ShapeDtypeStruct((feat, hidden), f32),
+            jax.ShapeDtypeStruct((board, feat), f32), out_shape[0], out_shape[1], out_shape[2], row_out, row_out, row_out,
+        ),
+        in_specs=[vmem] + [anywhere] * 4 + [in_hbm] * 2 + [anywhere] * 4,
+        out_specs=[anywhere] * 6 + [vmem] * 3,
+        scratch_shapes=[
+            pltpu.VMEM((2, total, half), bf16), like(neigh_weight), pltpu.VMEM((total, feat), f32),
+            like(embedding), like(child_grad), like(parent_grad),
+            pltpu.SemaphoreType.DMA((2 * chunks,)), pltpu.SemaphoreType.DMA, pltpu.SemaphoreType.DMA((3,)),
+            pltpu.SemaphoreType.DMA((chunks + 3,)),
+        ],
+        compiler_params=pltpu.CompilerParams(vmem_limit_bytes=K2_LIMIT << 20),
+    )(result[9], *result[3:7], *[pltpu.with_memory_space_constraint(x, pltpu.HBM) for x in result[7:9]], neigh_weight, embedding, child_grad, parent_grad)
+    return embedding, child_grad, parent_grad, proj_g, proj_b[0], neigh_g, neigh_b[0], comb_g, comb_b[0]
 
 
 def send(buffer):

time: 213 us -> 179 us (0.84)
  Pallas kernels: 195 us -> 178 us
  other arithmetic: 12.2 us -> 0 us
  local copies, waits for them, and re-layouts: 4.36 us -> 0.01 us
    pallas_call x1, Pallas kernels: 195 us -> 170 us  [fused(): pl.pallas_call(functools.partial(kernel, n, node), out_shape=out_shape, i...]
    convert_element_type x3 -> x0, other arithmetic: 10.8 us -> none  [the longest x1 6.78 us: fused(): comb_sum.astype(f32)]
    pallas_call x0 -> x1, Pallas kernels: none -> 7.99 us  [fused(): pl.pallas_call(widen, out_shape=(jax.ShapeDtypeStruct((2 * feat, feat), f...]
    unnamed x13 -> x2, local copies, waits for them, and re-layouts: 2.93 us -> 0.01 us
where the time goes in v2:
time: 179 us
  Pallas kernels  178 us (99%)
    pallas_call x1, Pallas kernels, fused(): pl.pallas_call(functools.partial(kernel, n, node), out_shape=out_shape, i...  170 us
    pallas_call x1, Pallas kernels, fused(): pl.pallas_call(widen, out_shape=(jax.ShapeDtypeStruct((2 * feat, feat), f...  7.99 us

profile of v2, /device:TPU:0, one launch (start us, length us, event | category | flops | bytes accessed | tf_op | source)
XLA Modules:
  0.0 178.5 jit_solution(14066119913109962189)
XLA Ops:
  0.6 0.0 copy-start
  0.7 169.7 %shard_map.196 = (bf16[512,1024]{1,0:T(8,128)(2,1)S(1)}, bf16[512,1024]{1,0:T(8,128)(2,1)S(1)}, bf16[512,1024]{1,0:T(8,128)(2,1)S(1)}, bf16[1024,512]{1,0:T(8,12...) custom-call(s32[4,128]{1,0:T(4,128)} %bitcast.16, ...), custom_call_target="tpu_custom_call" | custom-call | tf_op jit(solution)/shard_map/pallas_call | solution.py:554
  170.4 0.0 copy-done
  170.4 8.0 %shard_map.197 = (f32[2048,1024]{1,0:T(8,128)}, f32[1024,1024]{1,0:T(8,128)}, f32[512,1024]{1,0:T(8,128)}, bf16[512,1024]{1,0:T(8,128)(2,1)}, bf16[512,1024]{1,0...) custom-call(f32[16,1024]{1,0:T(8,128)S(1)} %get-tuple-element.28.bias_ref, ...), custom_call_target="tpu_custom_call" | custom-call | tf_op jit(solution)/shard_map/pallas_call | solution.py:596
Async XLA Ops:
  0.6 169.7 %copy-start = (bf16[1024,1024]{1,0:T(8,128)(2,1)S(1)}, bf16[1024,1024]{1,0:T(8,128)(2,1)}, u32[]{:S(2)}) copy-start(bf16[1024,1024]{1,0:T(8,128)(2,1)} %nw_h.3) | copy-start | bytes 6291460

commit v3 on v2

--- a/solution.py
+++ b/solution.py
@@ -11,18 +11,35 @@
 MESH = pl.DeviceIdType.MESH
 AXES = ("hop", "node")
 K2_LIMIT = 36
-X_FIRST = [[1], [2], [4], [8], [16]]
-Y_FIRST = [[1], [4], [2], [8], [16]]
-X_DIRECT = [[1], [2], [4], [8, 16]]
-Y_DIRECT = [[1], [4], [2], [8, 16]]
+WIDTHS = (256, 512, 256)
+NORM_UNROLL = 2
+COMBINE_UNROLL = 2
+
+
+def orders(halving, doubling=None):
+    return halving, doubling or halving[::-1]
+
+
+X_FIRST = orders([[1], [2], [4], [8], [16]])
+Y_FIRST = orders([[1], [4], [2], [8], [16]])
+X_DIRECT = orders([[1], [2], [4], [8, 16]])
+Y_DIRECT = orders([[1], [4], [2], [8, 16]])
+Z_DIRECT = orders([[1], [8, 16], [4], [2]])
 COMB_ORDERS = [X_FIRST, Y_FIRST] * 4
-TAIL_ORDERS = [X_DIRECT, Y_DIRECT, Y_DIRECT, X_DIRECT, Y_DIRECT, X_DIRECT]
+TAIL_ORDERS = [X_DIRECT, Z_DIRECT, Y_DIRECT] * 2 + [X_DIRECT, Y_DIRECT, X_DIRECT]
 PLAN = (
-    "S0", "S1", "G0", "c0", "G1", "c0", "c1", "G2", "c0", "c1", "c2", "G3", "BC", "P", "c0", "c1", "c2", "c3", "bc",
-    "A0", "c0", "c1", "c2", "c3", "A1", "BT", "c0", "c1", "c2", "c3", "n0", "n1", "I",
+    "S0", "S1", "S2", "G0", "c0", "G1", "c0", "c1", "G2", "c0", "c1", "c2", "G3", "BC", "P", "c0", "c1", "c2", "c3", "bc",
+    "A0", "c0", "c1", "c2", "c3", "A1", "c0", "n0", "A2", "BT", "c0", "c1", "c2", "c3", "n0", "n1", "n2", "I",
 )
-LATE = ("c0", "c1", "c2", "c3", "bc", "n0", "n1", "bt")
+LATE = ("c0", "c1", "c2", "c3", "bc", "n0", "n1", "n2", "bt")
 f32, bf16 = jnp.float32, jnp.bfloat16
+
+
+STARTS = tuple(sum(WIDTHS[:h]) for h in range(len(WIDTHS)))
+
+
+def wide_of(width):
+    return 256 if width % 256 == 0 else 128
 
 
 def dot(a, b):
@@ -42,12 +59,12 @@
     return sigma * (1.0 + value * (1.0 - sigma))
 
 
-def each(count, size, step):
+def each(count, size, step, unroll=1):
     def one(index, carry):
         step(pl.multiple_of(index * size, size))
         return carry
 
-    lax.fori_loop(0, count // size, one, 0)
+    lax.fori_loop(0, count // size, one, 0, unroll=unroll)
 
 
 class Net:
@@ -57,7 +74,16 @@
         self.bits = [1 << b for b in range(n.bit_length() - 1)]
         self.bit = {b: (self.me // b) % 2 for b in self.bits}
 
+        low = [b for b in self.bits if b < node]
+        self.outer = {m: self.joined(m * node, self.bits[len(low):]) // node for m in range(n // node)}
+        self.inner = {m: self.joined(m, low) for m in range(node)}
+
+    def joined(self, mask, bits):
+        return sum((1 - self.bit[b] if mask & b else self.bit[b]) * b for b in bits)
+
     def partner(self, mask):
+        if isinstance(mask, int):
+            return (self.outer[mask // self.node], self.inner[mask % self.node]), None
         index = 0
         for b in self.bits:
             index = index + ((self.bit[b] + (mask // b) % 2) % 2) * b
@@ -79,13 +105,15 @@
         return made
 
 
-def reduce_stream(net, sems, grad, landing, full, own_sem, first, rows, stages):
+def reduce_stream(net, sems, grad, landing, full, own_sem, first, rows, order):
+    stages, back = order
     off, length, land = 0, rows, first
-    trail = []
+    sizes = {}
     for bits in stages:
         ways = 1 << len(bits)
         part = length // ways
         mine = sum(net.bit[b] * (1 << i) for i, b in enumerate(bits))
+        sizes.update({b: part << i for i, b in enumerate(bits)})
         sent = []
         for c in range(1, ways):
             mask = sum(b for i, b in enumerate(bits) if (c >> i) & 1)
@@ -107,25 +135,32 @@
             grad[at, :] = total.astype(bf16)
 
         each(part, block, add)
-        trail.append((bits, off, length))
         off, length, land = keep, part, land + (ways - 1) * part
     source = grad.at[pl.ds(pl.multiple_of(first + off, 16), length)]
     own = pltpu.make_async_copy(source, full.at[pl.ds(pl.multiple_of(off, 16), length)], own_sem)
     own.start()
-    for bits, whole, size in reversed(trail):
-        at = full.at[pl.ds(pl.multiple_of(off, 16), length)]
-        if source is None:
-            source = at
+    done = []
+    for bits in back:
+        starts, run, apart = [sum(net.bit[b] * sizes[b] for b in sizes if b not in done)], length, []
+        for b in sorted(done, key=sizes.get):
+            if sizes[b] == run:
+                run *= 2
+            else:
+                apart.append(b)
+        for b in apart:
+            starts = starts + [start + sizes[b] for start in starts]
         sent = []
         for c in range(1, 1 << len(bits)):
             mask = sum(b for i, b in enumerate(bits) if (c >> i) & 1)
-            sent.append(sems.copy(source, at, net.partner(mask)[0]))
+            for start in starts:
+                at = full.at[pl.ds(pl.multiple_of(start, 16), run)]
+                sent.append(sems.copy(at if done else source, at, net.partner(mask)[0]))
         yield
-        if own is not None:
+        if not done:
             own.wait()
         for made in sent:
             made.wait()
-        off, length, source, own = whole, size, None, None
+        done = done + bits
 
 
 def bias_stream(net, sems, total, landing):
@@ -139,15 +174,16 @@
 def kernel(
     n, node,
     ct_h, cs_h, ps_h, im_h, bb_h, nb_h, cb_h, cf_h, pf_h, bp_h, nw_h, cw_h, og_h,
-    emb_h, cgr_h, pgr_h, c0_h, c1_h, c2_h, c3_h, n0_h, n1_h, bias_h,
+    emb_h, cgr_h, pgr_h, c0_h, c1_h, c2_h, c3_h, n0_h, n1_h, n2_h, bias_h,
     ct, cs, ps, im, bb, nb, cb, cf, pf, bp, nw, cw, og,
     mask, ci, slope, ng, pick, pick_t, spread, spread_t, inv,
-    out_f, in_f, in_b,
+    out_0, out_1, out_2, in_f0, in_f1, in_f2, in_b0, in_b1, in_b2,
     comb, agg, pf_t, left_t,
-    grad, landing, bias_c, bias_t, land_c, land_t,
+    grad, landing, g_n0, g_n1, g_n2, l_n0, l_n1, l_n2, bias_c, bias_t, land_c, land_t,
     in_sem, out_sem, own_sem, a_send, a_recv, r_send, r_recv,
 ):
-    pgr, cgr, gbd, agg_t, gnp, out_b, emb, gcomb = ng, pf, og, pick, spread_t, out_f, cf, ci
+    pgr, cgr, gbd, agg_t, gnp, emb, gcomb = ng, pf, og, pick, spread_t, cf, ci
+    out, in_f, in_b = (out_0, out_1, out_2), (in_f0, in_f1, in_f2), (in_b0, in_b1, in_b2)
     net = Net(n, node)
     sems = Sems(r_send, r_recv)
     me = net.me
@@ -161,11 +197,8 @@
 
     barrier = pltpu.get_barrier_semaphore()
 
-    def greet(i, carry):
-        pl.semaphore_signal(barrier, inc=1, device_id=net.partner(i)[0], device_id_type=MESH)
-        return carry
-
-    lax.fori_loop(1, n, greet, 0)
+    for other in range(n - 1, 0, -1):
+        pl.semaphore_signal(barrier, inc=1, device_id=net.partner(other)[0], device_id_type=MESH)
 
     loads = {}
     for i, (name, src, dst) in enumerate(
@@ -220,14 +253,14 @@
 
     a_order = n // 2
 
-    def send_all(out, into, h, which):
+    def send_all(into, h, which):
         def one(i, carry):
             far = i % 2 == 0
             m = jnp.where(far, n - 1 - i // 2, (i + 1) // 2)
             where, index = net.partner(m)
             pltpu.make_async_remote_copy(
-                src_ref=out.at[h, pl.ds(pl.multiple_of(index * cap, 16), cap)],
-                dst_ref=into.at[h, pl.ds(pl.multiple_of(me * cap, 16), cap)],
+                src_ref=out[h].at[pl.ds(pl.multiple_of(index * cap, 16), cap)],
+                dst_ref=into[h].at[pl.ds(pl.multiple_of(me * cap, 16), cap)],
                 send_sem=a_send.at[which], recv_sem=a_recv.at[which],
                 device_id=where, device_id_type=MESH,
             ).start()
@@ -235,23 +268,24 @@
 
         lax.fori_loop(0, n - 1, one, 0)
         own = pl.ds(pl.multiple_of(me * cap, 16), cap)
-        into[h, own, :] = out[h, own, :]
-
-    def all_of(out, into, h, which):
+        into[h][own, :] = out[h][own, :]
+
+    def all_of(into, h, which):
         return pltpu.make_async_remote_copy(
-            src_ref=out.at[h, pl.ds(0, edges - cap)], dst_ref=into.at[h, pl.ds(0, edges - cap)],
+            src_ref=out[h].at[pl.ds(0, edges - cap)], dst_ref=into[h].at[pl.ds(0, edges - cap)],
             send_sem=a_send.at[which], recv_sem=a_recv.at[which],
             device_id=net.partner(1)[0], device_id_type=MESH,
         )
 
-    for h in range(2):
+    for h, (start, width) in enumerate(zip(STARTS, WIDTHS)):
         def gather(c):
-            out_f[h, :, pl.ds(c, 256)] = dot(pick[...], ng[:, pl.ds(pl.multiple_of(h * half + c, 256), 256)]).astype(bf16)
-
-        each(half, 256, gather)
+            out[h][:, pl.ds(c, step)] = dot(pick[...], ng[:, pl.ds(pl.multiple_of(start + c, step), step)]).astype(bf16)
+
+        step = wide_of(width)
+        each(width, step, gather)
         if h == 0:
             pl.semaphore_wait(barrier, n - 1)
-        send_all(out_f, in_f, h, h)
+        send_all(in_f, h, h)
 
     for name in ("ps", "im", "cb"):
         loads[name].wait()
@@ -285,20 +319,21 @@
 
     each(children, 32, to_slope)
 
-    for h in range(2):
-        all_of(out_f, in_f, h, h).wait_recv()
+    for h, (start, width) in enumerate(zip(STARTS, WIDTHS)):
+        all_of(in_f, h, h).wait_recv()
 
         def aggregate(c):
-            sums = dot(spread_t[...], in_f[h, :, pl.ds(c, 256)]) * inv[...]
-            agg[:, pl.ds(pl.multiple_of(h * half + c, 256), 256)] = sums.astype(bf16)
-
-        each(half, 256, aggregate)
+            sums = dot(spread_t[...], in_f[h][:, pl.ds(c, step)]) * inv[...]
+            agg[:, pl.ds(pl.multiple_of(start + c, step), step)] = sums.astype(bf16)
+
+        step = wide_of(width)
+        each(width, step, aggregate)
 
         def combine(c):
             at = pl.ds(c, 256)
-            comb[:, at] += dot(agg[:, h * half : (h + 1) * half], cw[feat + h * half : feat + (h + 1) * half, at])
-
-        each(feat, 256, combine)
+            comb[:, at] += dot(agg[:, start : start + width], cw[feat + start : feat + start + width, at])
+
+        each(feat, 256, combine, COMBINE_UNROLL)
 
     bias_c[...] = jnp.zeros_like(bias_c)
 
@@ -307,17 +342,19 @@
         pre = comb[at, :]
         sigma = jax.nn.sigmoid(pre)
         z = pre * sigma
-        inverse = lax.rsqrt(jnp.sum(z * z, axis=1, keepdims=True) + epsilon)
+        gy = og[at, :].astype(f32)
+        squares = jnp.sum(z * z, axis=1, keepdims=True)
+        along = jnp.sum(z * gy, axis=1, keepdims=True)
+        inverse = lax.rsqrt(squares + epsilon)
         y = z * inverse
         emb[at, :] = y.astype(bf16)
-        gy = og[at, :].astype(f32)
-        gz = inverse * (gy - y * jnp.sum(y * gy, axis=1, keepdims=True))
+        gz = inverse * (gy - y * (inverse * along))
         g = (gz * (sigma * (1.0 + pre * (1.0 - sigma)))).astype(bf16)
         gcomb[at, :] = g
         wide_g = g.astype(f32)
         bias_c[...] += wide_g[0:8] + wide_g[8:16] + wide_g[16:24] + wide_g[24:32]
 
-    each(parents, 32, normalize)
+    each(parents, 32, normalize, NORM_UNROLL)
 
     stores = []
 
@@ -329,9 +366,10 @@
     groups = {}
     streams = []
 
-    sums = dict(c0=c0_h, c1=c1_h, c2=c2_h, c3=c3_h, n0=n0_h, n1=n1_h)
-
-    def begin(name, first, orders):
+    sums = dict(c0=c0_h, c1=c1_h, c2=c2_h, c3=c3_h, n0=n0_h, n1=n1_h, n2=n2_h)
+    child_grads, child_landing = (g_n0, g_n1, g_n2), (l_n0, l_n1, l_n2)
+
+    def begin(name, grad, landing, first, orders):
         groups[name] = []
         for i, stages in enumerate(orders):
             to = sums[name].at[pl.ds(512 * i, 512)]
@@ -348,13 +386,14 @@
 
     def send_back(h):
         def back(c):
-            at = pl.ds(pl.multiple_of(feat + h * half + c, 256), 256)
+            at = pl.ds(pl.multiple_of(feat + STARTS[h] + c, step), step)
             scaled = (times_transposed(gcomb[...], cw[at, :]) * inv[...]).astype(bf16)
-            out_b[h, :, pl.ds(c, 256)] = dot(spread[...], scaled).astype(bf16)
-
-        all_of(out_f, in_f, h, h).wait_send()
-        each(half, 256, back)
-        send_all(out_b, in_b, h, 2 + h)
+            out[h][:, pl.ds(c, step)] = dot(spread[...], scaled).astype(bf16)
+
+        all_of(in_f, h, h).wait_send()
+        step = wide_of(WIDTHS[h])
+        each(WIDTHS[h], step, back)
+        send_all(in_b, h, 3 + h)
 
     def comb_sum(k):
         h, part = k // 2, k % 2
@@ -368,7 +407,7 @@
             grad[pl.ds(base, feat), pl.ds(c, 256)] = dot(left[...], gcomb[:, at]).astype(bf16)
 
         each(half, 256, comb_grad)
-        begin("c%d" % k, base, COMB_ORDERS[2 * k : 2 * k + 2])
+        begin("c%d" % k, grad, landing, base, COMB_ORDERS[2 * k : 2 * k + 2])
 
     def parent_out():
         def parent_back(c):
@@ -379,18 +418,18 @@
         store(pgr, pgr_h)
 
     def child_sum(h):
-        all_of(out_b, in_b, h, 2 + h).wait_recv()
-        first = 4 * feat + h * (feat + board)
+        all_of(in_b, h, 3 + h).wait_recv()
 
         def child_back(c):
-            at = pl.ds(pl.multiple_of(h * half + c, 256), 256)
-            grown = dot(pick_t[...], in_b[h, :, pl.ds(c, 256)])
+            at = pl.ds(pl.multiple_of(STARTS[h] + c, step), step)
+            grown = dot(pick_t[...], in_b[h][:, pl.ds(c, step)])
             g = (grown * slope[:, at]).astype(bf16)
             gnp[:, at] = g
-            grad[pl.ds(first, feat + board), pl.ds(c, 256)] = dot(left_t[...], g).astype(bf16)
-
-        each(half, 256, child_back)
-        begin("n%d" % h, first, TAIL_ORDERS[3 * h : 3 * h + 3])
+            child_grads[h][:, pl.ds(c, step)] = dot(left_t[...], g).astype(bf16)
+
+        step = wide_of(WIDTHS[h])
+        each(WIDTHS[h], step, child_back)
+        begin("n%d" % h, child_grads[h], child_landing[h], 0, TAIL_ORDERS[3 * h : 3 * h + 3])
 
     def bias_sum(name, total, landing_rows):
         groups[name] = [bias_stream(net, sems, total, landing_rows)]
@@ -427,9 +466,9 @@
         store(cgr, cgr_h)
 
     tasks = {
-        "S0": lambda: send_back(0), "S1": lambda: send_back(1),
+        "S0": lambda: send_back(0), "S1": lambda: send_back(1), "S2": lambda: send_back(2),
         "G0": lambda: comb_sum(0), "G1": lambda: comb_sum(1), "G2": lambda: comb_sum(2), "G3": lambda: comb_sum(3),
-        "A0": lambda: child_sum(0), "A1": lambda: child_sum(1),
+        "A0": lambda: child_sum(0), "A1": lambda: child_sum(1), "A2": lambda: child_sum(2),
         "BC": lambda: bias_sum("bc", bias_c, land_c), "BT": child_biases, "P": parent_out, "I": child_out,
     }
     for token in PLAN:
@@ -443,14 +482,14 @@
 
     bias_h[0:8, :] = bias_c[...]
     bias_h[8:16, :] = bias_t[...]
-    for h in range(2):
-        all_of(out_b, in_b, h, 2 + h).wait_send()
+    for h in range(3):
+        all_of(in_b, h, 3 + h).wait_send()
     for made in stores:
         made.wait()
 
 
 def widen(
-    bias_ref, c0_h, c1_h, c2_h, c3_h, n0_h, n1_h, nw_h, emb_h, cgr_h, pgr_h,
+    bias_ref, c0_h, c1_h, c2_h, c3_h, n0_h, n1_h, n2_h, nw_h, emb_h, cgr_h, pgr_h,
     comb_o, neigh_o, proj_o, emb_o, cgr_o, pgr_o, comb_b, neigh_b, proj_b,
     sums, nw, wide, emb, cgr, pgr, sum_sem, nw_sem, row_sem, out_sem,
 ):
@@ -463,13 +502,16 @@
     def piece(i):
         if i < 2 * per:
             at = pl.ds((i % per) * block, block)
-            return [(c0_h, c1_h)[i // per].at[at], (c2_h, c3_h)[i // per].at[at]]
+            return [(0, half, (c0_h, c1_h)[i // per].at[at]), (half, half, (c2_h, c3_h)[i // per].at[at])]
         at = pl.ds((i - 2 * per) * block, block)
-        return [n0_h.at[at], n1_h.at[at]]
-
-    chunks = [pl.ds(i * block, block) for i in range(sums.shape[1] // block)]
+        return [(start, width, n.at[at]) for start, width, n in zip(STARTS, WIDTHS, (n0_h, n1_h, n2_h))]
+
+    chunks = [pl.ds(i * block, block) for i in range(sums.shape[0] // block)]
     loads = [
-        [pltpu.make_async_copy(src, sums.at[h, at], sum_sem.at[2 * i + h]) for h, src in enumerate(piece(i))]
+        [
+            pltpu.make_async_copy(src, sums.at[at, pl.ds(start, width)], sum_sem.at[3 * i + h])
+            for h, (start, width, src) in enumerate(piece(i))
+        ]
         for i, at in enumerate(chunks)
     ]
     load_nw = pltpu.make_async_copy(nw_h, nw, nw_sem)
@@ -488,30 +530,38 @@
     for made, (_, mid, dst) in zip(row_loads, rows):
         made.wait()
         store(mid, dst)
-    for i, at in enumerate(chunks):
+    def widened(i):
+        at = chunks[i]
         for made in loads[i]:
             made.wait()
-        if i * block < 3 * feat:
-            for h in range(2):
-                wide[at, h * half : (h + 1) * half] = sums[h, at, :].astype(f32)
-            if i * block < 2 * feat:
-                store(wide.at[at], comb_o.at[at])
-            else:
-                store(wide.at[at], neigh_o.at[pl.ds(i * block - 2 * feat, block)])
+        if i * block >= 3 * feat:
+            wide[at, :] = times_transposed(sums[at, :], nw[...])
+            store(wide.at[at], proj_o.at[pl.ds(i * block - 3 * feat, block)])
+            return
+        wide[at, :] = sums[at, :].astype(f32)
+        if i * block < 2 * feat:
+            store(wide.at[at], comb_o.at[at])
+        else:
+            store(wide.at[at], neigh_o.at[pl.ds(i * block - 2 * feat, block)])
+
+    before = len(chunks) // 2
+    for i in range(before):
+        widened(i)
     load_nw.wait()
-    for r in range(0, board, block):
-        at = pl.ds(3 * feat + r, block)
-        wide[at, :] = times_transposed(sums[0, at, :], nw[:, 0:half]) + times_transposed(sums[1, at, :], nw[:, half:])
-        store(wide.at[at], proj_o.at[pl.ds(r, block)])
+    for i in range(3 * feat // block, len(chunks)):
+        widened(i)
+    for i in range(before, 3 * feat // block):
+        widened(i)
     comb_b[...] = jnp.sum(bias_ref[0:8, :], axis=0, keepdims=True)
     neigh_b[...] = bias_ref[8:9, :]
-    line = jnp.broadcast_to(bias_ref[9:10, :], (16, feat))
+    line = bias_ref[9:10, :]
     high = line.astype(bf16)
     rest = line - high.astype(f32)
     low = rest.astype(bf16)
     lowest = (rest - low.astype(f32)).astype(bf16)
-    parts = [times_transposed(x, nw[...]) for x in (high, low, lowest)]
-    proj_b[...] = (parts[0] + (parts[1] + parts[2]))[0:1]
+    parts = jnp.concatenate([jnp.broadcast_to(x.astype(f32), (8, feat)) for x in (high, low, lowest, lowest)], axis=0)
+    spun = times_transposed(parts.astype(bf16), nw[...])
+    proj_b[...] = spun[0:1] + (spun[8:9] + spun[16:17])
     for made in stores:
         made.wait()
 
@@ -538,24 +588,25 @@
     )
     half = hidden // 2
     steps = n.bit_length() - 1
-    grads = pltpu.VMEM((6 * feat + 2 * board, half), bf16)
-    messages = pltpu.VMEM((2, edges, half), bf16)
+    grads = pltpu.VMEM((4 * feat, half), bf16)
+    child_grads = [pltpu.VMEM((feat + board, width), bf16) for width in WIDTHS]
+    messages = [pltpu.VMEM((edges, width), bf16) for width in WIDTHS]
     row = pltpu.VMEM((8, feat), f32)
     rows = pltpu.VMEM((steps, 8, feat), f32)
-    copies = 14 * 14 + 2 * steps
+    copies = 17 * 20 + 2 * steps
     out_shape = (
         jax.ShapeDtypeStruct((parents, feat), bf16),
         jax.ShapeDtypeStruct((children, feat), bf16),
         jax.ShapeDtypeStruct((parents, feat), bf16),
         *[jax.ShapeDtypeStruct((feat, half), bf16)] * 4,
-        *[jax.ShapeDtypeStruct((feat + board, half), bf16)] * 2,
+        *[jax.ShapeDtypeStruct((feat + board, width), bf16) for width in WIDTHS],
         jax.ShapeDtypeStruct((16, feat), f32),
     )
     result = pl.pallas_call(
         functools.partial(kernel, n, node),
         out_shape=out_shape,
         in_specs=[in_hbm] * 13,
-        out_specs=[anywhere] * 9 + [vmem],
+        out_specs=[anywhere] * 10 + [vmem],
         scratch_shapes=[
             *[like(x) for x in small],
             like(child_features), like(parent_features), like(board_proj), like(neigh_weight), like(comb_weight), like(out_grad),
@@ -568,17 +619,17 @@
             pltpu.VMEM((edges, parents), bf16),
             pltpu.VMEM((parents, edges), bf16),
             pltpu.VMEM((parents, 1), f32),
-            messages, messages, messages,
+            *messages, *messages, *messages,
             pltpu.VMEM((parents, feat), f32),
             pltpu.VMEM((parents, hidden), bf16),
             pltpu.VMEM((feat, parents), bf16),
             pltpu.VMEM((feat + board, children), bf16),
-            grads, grads, row, row, rows, rows,
+            grads, grads, *child_grads, *child_grads, row, row, rows, rows,
             pltpu.SemaphoreType.DMA((13,)),
             pltpu.SemaphoreType.DMA((3,)),
-            pltpu.SemaphoreType.DMA((14,)),
-            pltpu.SemaphoreType.DMA((4,)),
-            pltpu.SemaphoreType.DMA((4,)),
+            pltpu.SemaphoreType.DMA((17,)),
+            pltpu.SemaphoreType.DMA((6,)),
+            pltpu.SemaphoreType.DMA((6,)),
             pltpu.SemaphoreType.DMA((copies,)),
             pltpu.SemaphoreType.DMA((copies,)),
         ],
@@ -590,6 +641,7 @@
         child_features, parent_features, board_proj, neigh_weight, comb_weight, out_grad,
     )
     embedding, child_grad, parent_grad = result[:3]
+    hold = functools.partial(pltpu.with_memory_space_constraint, memory_space=pltpu.HBM)
     row_out = jax.ShapeDtypeStruct((1, feat), f32)
     total = 3 * feat + board
     chunks = total // 512
@@ -599,16 +651,16 @@
             jax.ShapeDtypeStruct((2 * feat, feat), f32), jax.ShapeDtypeStruct((feat, hidden), f32),
             jax.ShapeDtypeStruct((board, feat), f32), out_shape[0], out_shape[1], out_shape[2], row_out, row_out, row_out,
         ),
-        in_specs=[vmem] + [anywhere] * 4 + [in_hbm] * 2 + [anywhere] * 4,
+        in_specs=[vmem] + [anywhere] * 11,
         out_specs=[anywhere] * 6 + [vmem] * 3,
         scratch_shapes=[
-            pltpu.VMEM((2, total, half), bf16), like(neigh_weight), pltpu.VMEM((total, feat), f32),
+            pltpu.VMEM((total, feat), bf16), like(neigh_weight), pltpu.VMEM((total, feat), f32),
             like(embedding), like(child_grad), like(parent_grad),
-            pltpu.SemaphoreType.DMA((2 * chunks,)), pltpu.SemaphoreType.DMA, pltpu.SemaphoreType.DMA((3,)),
+            pltpu.SemaphoreType.DMA((3 * chunks,)), pltpu.SemaphoreType.DMA, pltpu.SemaphoreType.DMA((3,)),
             pltpu.SemaphoreType.DMA((chunks + 3,)),
         ],
         compiler_params=pltpu.CompilerParams(vmem_limit_bytes=K2_LIMIT << 20),
-    )(result[9], *result[3:7], *[pltpu.with_memory_space_constraint(x, pltpu.HBM) for x in result[7:9]], neigh_weight, embedding, child_grad, parent_grad)
+    )(result[10], *result[3:6], hold(result[6]), result[7], hold(result[8]), result[9], neigh_weight, embedding, child_grad, parent_grad)
     return embedding, child_grad, parent_grad, proj_g, proj_b[0], neigh_g, neigh_b[0], comb_g, comb_b[0]
 
 

time: 179 us -> 174 us (0.972)
  Pallas kernels: 178 us -> 173 us
    pallas_call x1, Pallas kernels: 170 us -> 165 us  [fused(): pl.pallas_call(functools.partial(kernel, n, node), out_shape=out_shape, i...]
where the time goes in v3:
time: 174 us
  Pallas kernels  173 us (99%)
    pallas_call x1, Pallas kernels, fused(): pl.pallas_call(functools.partial(kernel, n, node), out_shape=out_shape, i...  165 us
    pallas_call x1, Pallas kernels, fused(): pl.pallas_call(widen, out_shape=(jax.ShapeDtypeStruct((2 * feat, feat), f...  8.58 us

profile of v3, /device:TPU:0, one launch (start us, length us, event | category | flops | bytes accessed | tf_op | source)
XLA Modules:
  0.0 174.2 jit_solution(528846784807783773)
XLA Ops:
  0.6 0.0 copy-start
  0.7 164.8 %shard_map.196 = (bf16[512,1024]{1,0:T(8,128)(2,1)S(1)}, bf16[512,1024]{1,0:T(8,128)(2,1)S(1)}, bf16[512,1024]{1,0:T(8,128)(2,1)S(1)}, bf16[1024,512]{1,0:T(8,12...) custom-call(s32[4,128]{1,0:T(4,128)} %bitcast.16, ...), custom_call_target="tpu_custom_call" | custom-call | tf_op jit(solution)/shard_map/pallas_call | solution.py:605
  165.4 0.0 copy-done
  165.4 8.6 %shard_map.197 = (f32[2048,1024]{1,0:T(8,128)}, f32[1024,1024]{1,0:T(8,128)}, f32[512,1024]{1,0:T(8,128)}, bf16[512,1024]{1,0:T(8,128)(2,1)}, bf16[512,1024]{1,0...) custom-call(f32[16,1024]{1,0:T(8,128)S(1)} %get-tuple-element.29.bias_ref, ...), custom_call_target="tpu_custom_call" | custom-call | tf_op jit(solution)/shard_map/pallas_call | solution.py:648
Async XLA Ops:
  0.6 164.8 %copy-start = (bf16[1024,1024]{1,0:T(8,128)(2,1)S(1)}, bf16[1024,1024]{1,0:T(8,128)(2,1)}, u32[]{:S(2)}) copy-start(bf16[1024,1024]{1,0:T(8,128)(2,1)} %nw_h.3) | copy-start | bytes 6291460
